TPU v7x, 256 devices: a whole 4x4x8 slice. The times are simulated.
256 devices in a mesh: pole: 4 (over y), row: 8 (over z), col: 8 (over x, core).
Axes of the slice: x: 4, y: 4, z: 8, core: 2. Of those that a mesh axis runs over, the one named last changes fastest.
Arguments:
- root_inverse: float32 [8, 1024, 1024], P('pole', ('row', 'col')), may hold values from -100 to 100
- node_factor: float32 [8, 8, 1024, 512], P('pole', 'row', None, 'col'), may hold values from -0.1875 to 0.1875
- node_inverse: float32 [8, 8, 512, 512], P('pole', 'row'), may hold values from -100 to 100
- leaf_root_factor: float32 [8, 64, 1024, 256], P('pole', ('row', 'col')), may hold values from -0.1875 to 0.1875
- leaf_node_factor: float32 [8, 64, 512, 256], P('pole', ('row', 'col')), may hold values from -0.25 to 0.25
- leaf_inverse: float32 [8, 64, 256, 256], P('pole', ('row', 'col')), may hold values from -100 to 100
- leaf_pattern: int32 [64, 8], P(('row', 'col')), may hold values 0 or 1
- pole_weight: float32 [8], P('pole'), may hold values from 0.1 to 1
Outputs:
- root_block: float32 [1024, 1024], P(('row', 'col'))
- node_offdiag: float32 [8, 1024, 512], P('row', None, 'col')
- node_diag: float32 [8, 512, 512], P('row', 'col')
- leaf_root: float32 [64, 1024, 256], P(('row', 'col'))
- leaf_node: float32 [64, 512, 256], P(('row', 'col'))
- leaf_diag: float32 [64, 256, 256], P(('row', 'col'))
All inputs are finite; a program needn't handle non-finite values. No bound on the sum of `leaf_pattern` on one device may be relied on, other than what follows from the above.
Results may differ from a plain program's by a relative error of at most 0.0001.
Values sent between devices are 32-bit elements; how exact they have to be, the bound alone decides.
A program may use at most 64 MiB of HBM per device.

v0:
```python
import jax
import jax.numpy as jnp
from jax import lax
from jax.sharding import PartitionSpec as P

highest = lax.Precision.HIGHEST


def product(left, right):
    return jnp.matmul(left, right, precision=highest)


def weighted(weights, values):
    return jnp.sum(weights[:, None, None] * values, axis=0)


def shards(
    root_inverse,
    node_factor,
    node_inverse,
    leaf_root_factor,
    leaf_node_factor,
    leaf_inverse,
    leaf_pattern,
    pole_weight,
):
    node_cols = node_factor[:, 0]
    node_inv = node_inverse[:, 0]
    node_leaf = leaf_node_factor[:, 0]
    leaf_inv = leaf_inverse[:, 0]
    block_rows = leaf_root_factor.shape[2] // leaf_pattern.shape[1]
    row_mask = jnp.repeat(leaf_pattern[0].astype(jnp.float32), block_rows)
    root_leaf = leaf_root_factor[:, 0] * row_mask[None, :, None]
    width = node_cols.shape[2]
    joined = jnp.concatenate([node_cols, root_leaf], axis=2)
    products = product(lax.all_gather(root_inverse, ("row", "col"), axis=1, tiled=True), joined)
    offdiag = -products[:, :, :width]
    root_times = products[:, :, width:]
    col_index = lax.axis_index("col")
    own_rows = lax.dynamic_slice_in_dim(node_inv, col_index * width, width, 1)
    factor_t = jnp.swapaxes(node_cols, 1, 2)
    piece = lax.all_gather(offdiag, "col", axis=2, tiled=True)
    root_sum = root_times
    root_sum = root_sum + product(piece, node_leaf)
    node_part = product(jnp.swapaxes(piece, 1, 2), root_leaf)
    cross = product(factor_t, piece)
    root_sum, node_part, cross = (root_sum, node_part, cross)
    diag_rows = own_rows - cross
    diag_times = product(lax.all_gather(diag_rows, "col", axis=1, tiled=True), node_leaf)
    upper_levels = (
        weighted(pole_weight, root_inverse),
        weighted(pole_weight, offdiag)[None],
        weighted(pole_weight, diag_rows)[None],
    )
    middle_part = node_part + diag_times
    lower_part = (
        leaf_inv
        + product(jnp.swapaxes(root_leaf, 1, 2), root_sum)
        + product(jnp.swapaxes(node_leaf, 1, 2), middle_part)
    )
    leaf_levels = (
        weighted(pole_weight, -root_sum)[None],
        weighted(pole_weight, -middle_part)[None],
        weighted(pole_weight, lower_part)[None],
    )
    totals = lax.psum(
        (
            upper_levels[0],
            upper_levels[1],
            upper_levels[2],
            leaf_levels[0],
            leaf_levels[1],
            leaf_levels[2],
        ),
        "pole",
    )
    return (totals[0], totals[1], totals[2], totals[3], totals[4], totals[5])


def solution(mesh):
    return jax.shard_map(
        shards,
        mesh=mesh,
        in_specs=(
            P("pole", ("row", "col"), None),
            P("pole", "row", None, "col"),
            P("pole", "row", None, None),
            P("pole", ("row", "col"), None, None),
            P("pole", ("row", "col"), None, None),
            P("pole", ("row", "col"), None, None),
            P(("row", "col"), None),
            P("pole"),
        ),
        out_specs=(
            P(("row", "col"), None),
            P("row", None, "col"),
            P("row", "col", None),
            P(("row", "col"), None, None),
            P(("row", "col"), None, None),
            P(("row", "col"), None, None),
        ),
        check_vma=False,
    )
```

profile of v0, /device:TPU:6, one launch (start us, length us, event | category | flops | bytes accessed | tf_op | source)
XLA Modules:
  0.0 271.1 jit_solution(6661913665170530114)
XLA Ops:
  7.2 0.7 all-gather.4.cloned.1.call-update
  8.0 2.9 %copy.20 = f32[2,1,1024,256]{2,3,0,1:T(8,128)} copy(f32[2,1,1024,256]{3,2,1,0:T(8,128)} %param.11) | data formatting | bytes 4194304 | tf_op args[3]
  11.0 1.8 bitcast_multiply_fusion
  12.8 82.0 %all-gather.4.cloned.1.call-done = f32[2,1024,1024]{2,1,0:T(8,128)} async-done(((f32[2,16,1024]{2,1,0:T(8,128)}), f32[2,1024,1024]{2,1,0:T(8,128)}) %all-gather.4.cloned.1.call-update) | async-done | bytes 8388624 | tf_op jit(solution)/shard_map/all_gather | solution.py:36
  94.8 11.3 %fusion.4 = f32[2,1024,320]{1,2,0:T(8,128)S(1)} fusion(f32[2,1024,1024]{2,1,0:T(8,128)} %all-gather.4.cloned.1.call-done, f32[2,1024,256]{1,2,0:T(8,128)S(1)} %bitcast_multiply_fusion, f32[2,1024,64]{1,2,0:T(8,128)} %bitcast.54), kind=kOutput, calls=%fused_computation.7 | convolution fusion | flops 8053719040 | bytes 13631488 | tf_op jit(solution)/shard_map/dot_general | solution.py:10
  106.2 1.5 copy-done.2
  107.7 1.6 slice_negate_fusion
  109.4 31.9 %all-gather.6.cloned.1.call-done = f32[2,1024,512]{1,2,0:T(8,128)} async-done(((f32[2,1024,64]{1,2,0:T(8,128)}), f32[2,1024,512]{1,2,0:T(8,128)}) %all-gather.6.cloned.1.call-update) | async-done | bytes 4194320 | tf_op jit(solution)/shard_map/all_gather | solution.py:42
  141.3 7.9 %multiply_reduce_fusion.3 = (f32[64,512]{1,0:T(8,128)}, f32[2,64,512]{2,1,0:T(8,128)}) fusion(f32[2]{0:T(128)S(1)} %copy-done.11, f32[2,1024,512]{1,2,0:T(8,128)} %all-gather.6.cloned.1.call-done, f32[2,1,1024,64]{2,3,1,0:T(8,128)} %param.9, f32[2,1,512,512]{3,2,1,0:T(8,128)} %param.10, s32[]{:T(128)S(6)} %select_n.3), kind=kOutput, calls=%fused_computation.23 | convolution fusion | flops 805470208 | bytes 5373964 | tf_op jit(solution)/shard_map/dot_general | solution.py:10
  149.2 0.2 all-reduce.3.cloned.1.call-start
  149.5 0.7 multiply_reduce_fusion.4
  150.2 8.0 %multiply_reduce_fusion = (f32[1024,256]{0,1:T(8,128)}, f32[2,1024,256]{1,2,0:T(8,128)S(1)}) fusion(f32[2]{0:T(128)S(1)} %copy-done.11, f32[2,1024,512]{1,2,0:T(8,128)} %all-gather.6.cloned.1.call-done, f32[2,1,512,256]{3,2,1,0:T(8,128)S(1)} %copy-done, f32[2,1024,320]{1,2,0:T(8,128)} %copy-done.2), kind=kOutput, calls=%fused_computation.6 | convolution fusion | flops 3223060480 | bytes 10485768 | tf_op jit(solution)/shard_map/dot_general | solution.py:10
  158.1 2.9 %convolution_add_fusion.1 = f32[2,256,256]{2,1,0:T(8,128)} fusion(f32[2,1024,256]{1,2,0:T(8,128)S(1)} %bitcast_multiply_fusion, f32[2,1024,256]{1,2,0:T(8,128)S(1)} %get-tuple-element.23, f32[2,1,256,256]{3,2,1,0:T(8,128)S(1)} %copy-done.4), kind=kOutput, calls=%fused_computation.11 | convolution fusion | flops 1610743808 | bytes 5242880 | tf_op jit(solution)/shard_map/dot_general | solution.py:10
  161.1 16.9 %all-gather.8.cloned.1.call-done = f32[2,512,512]{2,1,0:T(8,128)} async-done(((f32[2,64,512]{2,1,0:T(8,128)}), f32[2,512,512]{2,1,0:T(8,128)}) %all-gather.8.cloned.1.call-update) | async-done | bytes 2097168 | tf_op jit(solution)/shard_map/all_gather | solution.py:49
  178.0 3.7 %fusion.12 = f32[2,512,256]{2,1,0:T(8,128)S(1)} fusion(f32[2,512,512]{2,1,0:T(8,128)} %all-gather.8.cloned.1.call-done, f32[2,1,512,256]{3,2,1,0:T(8,128)S(1)} %copy-done), kind=kOutput, calls=%fused_computation.17 | convolution fusion | flops 1610612736 | bytes 4194304 | tf_op jit(solution)/shard_map/dot_general | solution.py:10
  181.7 4.7 %multiply_reduce_fusion.1 = (f32[512,256]{1,0:T(8,128)}, f32[2,512,256]{2,1,0:T(8,128)S(1)}) fusion(f32[2]{0:T(128)S(1)} %copy-done.11, f32[2,512,256]{2,1,0:T(8,128)S(1)} %fusion.12, f32[2,1024,512]{1,2,0:T(8,128)S(1)} %copy-done.1, f32[2,1024,256]{1,2,0:T(8,128)S(1)} %bitcast_multiply_fusion), kind=kOutput, calls=%fused_computation.20 | convolution fusion | flops 3222142976 | bytes 8912904 | tf_op jit(solution)/shard_map/dot_general | solution.py:10
  186.4 2.6 fusion.9
  189.0 69.4 %all-reduce.3.cloned.1.call-done = (f32[16,1024]{1,0:T(8,128)}, f32[1,1024,64]{1,2,0:T(8,128)}, f32[1,64,512]{2,1,0:T(8,128)}, f32[1,1024,256]{1,2,0:T(8,128)}, ...) async-done(((f32[16,1024]{1,0:T(8,128)}, f32[1,1024,64]{1,2,0:T(8,128)}, f32[1,64,512]{2,1,0:T(8,128)}, f32[1,1024,256]{1,2,0:T(8,128)}, f32[1,512,256]{2,1,0:T(8,128)}, ...) | async-done | bytes 2293776 | tf_op jit(solution)/shard_map/psum | solution.py:66
  258.4 2.6 copy.26
  261.0 0.6 copy.38
  261.7 0.7 copy.39
  262.4 0.7 copy.40
  263.0 0.8 copy.41
  263.8 0.7 copy.42
  (33 shorter events, 0.3 us)
Async XLA Ops:
  7.2 143.0 %copy-start = (f32[2,1,512,256]{3,2,1,0:T(8,128)S(1)}, f32[2,1,512,256]{3,2,1,0:T(8,128)}, u32[]{:S(2)}) copy-start(f32[2,1,512,256]{3,2,1,0:T(8,128)} %param.12) | copy-start | bytes 3145732
  7.2 87.7 %all-gather.4.cloned.1.call-start = ((), (), s32[]{:S(2)}) async-start(), calls=%async_computation | async-start | bytes 8519680 | tf_op jit(solution)/shard_map/all_gather | solution.py:36
  7.9 3.0 %copy-start.12 = (s32[1,8]{1,0:T(1,128)S(1)}, s32[1,8]{1,0:T(1,128)}, u32[]{:S(2)}) copy-start(s32[1,8]{1,0:T(1,128)} %param.14) | copy-start | bytes 100
  7.9 133.4 %all-gather.6.cloned.1.call-start = ((), (), s32[]{:S(2)}) async-start(), calls=%async_computation.1 | async-start | bytes 4718592 | tf_op jit(solution)/shard_map/all_gather | solution.py:42
  94.8 12.9 %copy-start.11 = (f32[2]{0:T(128)S(1)}, f32[2]{0:T(128)}, u32[]{:S(2)}) copy-start(f32[2]{0:T(128)} %param.15) | copy-start | bytes 28
  106.2 1.5 copy-start.2
  109.3 68.7 %all-gather.8.cloned.1.call-start = ((), (), s32[]{:S(2)}) async-start(), calls=%async_computation.2 | async-start | bytes 2359296 | tf_op jit(solution)/shard_map/all_gather | solution.py:49
  109.4 40.1 %copy-start.6 = (f32[2,16,1024]{2,1,0:T(8,128)S(1)}, f32[2,16,1024]{2,1,0:T(8,128)}, u32[]{:S(2)}) copy-start(f32[2,16,1024]{2,1,0:T(8,128)} %param.8) | copy-start | bytes 393220
  149.2 109.1 %all-reduce.3.cloned.1.call-start = ((), (), s32[]{:S(2)}) async-start(), calls=%async_computation.3 | async-start | bytes 4587520 | tf_op jit(solution)/shard_map/psum | solution.py:66
  150.2 8.0 %copy-start.4 = (f32[2,1,256,256]{3,2,1,0:T(8,128)S(1)}, f32[2,1,256,256]{3,2,1,0:T(8,128)}, u32[]{:S(2)}) copy-start(f32[2,1,256,256]{3,2,1,0:T(8,128)} %param.13) | copy-start | bytes 1572868
  178.0 3.7 %copy-start.1 = (f32[2,1024,512]{1,2,0:T(8,128)S(1)}, f32[2,1024,512]{1,2,0:T(8,128)}, u32[]{:S(2)}) copy-start(f32[2,1024,512]{1,2,0:T(8,128)} %all-gather.6.cloned.1.call-done) | copy-start | bytes 12582916
  181.7 4.7 %copy-start.3 = (f32[2,256,256]{2,1,0:T(8,128)S(1)}, f32[2,256,256]{2,1,0:T(8,128)}, u32[]{:S(2)}) copy-start(f32[2,256,256]{2,1,0:T(8,128)} %convolution_add_fusion.1) | copy-start | bytes 1572868
  258.4 2.6 copy-start.10
  258.4 3.3 %copy-start.8 = (f32[1,1024,64]{1,2,0:T(8,128)S(1)}, f32[1,1024,64]{1,2,0:T(8,128)}, u32[]{:S(2)}) copy-start(f32[1,1024,64]{1,2,0:T(8,128)} %get-tuple-element.27) | copy-start | bytes 786436
  258.4 4.0 %copy-start.9 = (f32[1,64,512]{2,1,0:T(8,128)S(1)}, f32[1,64,512]{2,1,0:T(8,128)}, u32[]{:S(2)}) copy-start(f32[1,64,512]{2,1,0:T(8,128)} %get-tuple-element.28) | copy-start | bytes 393220
  258.4 4.6 %copy-start.5 = (f32[1,512,256]{2,1,0:T(8,128)S(1)}, f32[1,512,256]{2,1,0:T(8,128)}, u32[]{:S(2)}) copy-start(f32[1,512,256]{2,1,0:T(8,128)} %get-tuple-element.30) | copy-start | bytes 1572868
  258.4 5.4 %copy-start.7 = (f32[1,256,256]{2,1,0:T(8,128)S(1)}, f32[1,256,256]{2,1,0:T(8,128)}, u32[]{:S(2)}) copy-start(f32[1,256,256]{2,1,0:T(8,128)} %get-tuple-element.31) | copy-start | bytes 786436
Sparse Core Ops, SparseCore 0:
  10.8 83.9 all-gather.3
  109.4 31.8 all-gather.5
  149.4 28.5 all-gather.7
  189.1 69.2 all-reduce.2
where the time goes:
time: 272 us; the launch traced here: 271 us
  waiting for transfers between devices  201 us (74%)
  matrix products  41 us (15%)
  between operations  13.9 us (5%)
  local copies, waits for them, and re-layouts  10.7 us (4%)
  other arithmetic  4.09 us (2%)
    all_gather x1, waiting for transfers between devices, shards(): lax.all_gather(root_inverse, ('row', 'col'), axis=1, tiled=True)  82 us
    psum x1, waiting for transfers between devices, shards(): lax.psum((upper_levels[0], upper_levels[1], upper_levels[2], leaf_levels[...  69.4 us
    dot_general x7, matrix products, product(): return jnp.matmul(left, right, precision=highest)  41 us
    all_gather x1, waiting for transfers between devices, shards(): piece = lax.all_gather(offdiag, 'col', axis=2, tiled=True)  31.9 us
    all_gather x1, waiting for transfers between devices, shards(): lax.all_gather(diag_rows, 'col', axis=1, tiled=True)  16.9 us
    unnamed x33, local copies, waits for them, and re-layouts  10.6 us
  transfers between devices with their start and end apart: 4, of which 4 were waited for; matrix products, arithmetic and copies ran while one was open for 6% of the time, Pallas kernels for 0%

commit v1 on v0

v1 whole, which is shorter than its diff:
```python
import functools

import jax
import jax.numpy as jnp
from jax import lax
from jax.experimental import pallas as pl
from jax.experimental.pallas import tpu as pltpu
from jax.sharding import PartitionSpec as P

high = lax.Precision.HIGH
MESH = pl.DeviceIdType.MESH


def product(left, right):
    return jnp.matmul(left, right, precision=high)


def weighted(weights, values):
    return jnp.sum(weights[:, None, None] * values, axis=0)


def gather_kernel(
    n_row, n_x, r_ref, f_ref, rg, fg,
    near_send, near_recv, ring_send, ring_recv, pair_send, pair_recv,
    wide_send, wide_recv, mate_send, mate_recv, local_sem,
):
    pole, row, col = lax.axis_index("pole"), lax.axis_index("row"), lax.axis_index("col")
    x, core = col // 2, lax.rem(col, 2)
    other = 1 - core

    def at(dx, k):
        return (pole, row, lax.rem(x + dx + n_x, n_x) * 2 + k)

    up = (pole, lax.rem(row + 1, n_row), col)
    down = (pole, lax.rem(row + n_row - 1, n_row), col)
    mate = (pole, row, x * 2 + other)

    barrier = pltpu.get_barrier_semaphore()
    peers = [up, down, mate] + [at(dx, k) for dx in range(1, n_x) for k in range(2)]
    for peer in peers:
        pl.semaphore_signal(barrier, inc=1, device_id=peer, device_id_type=MESH)
    pl.semaphore_wait(barrier, len(peers))

    def remote(src, dst, ssem, rsem, dev):
        return pltpu.make_async_remote_copy(
            src_ref=src, dst_ref=dst, send_sem=ssem, recv_sem=rsem,
            device_id=dev, device_id_type=MESH,
        )

    own = pl.ds(pl.multiple_of(col * 16, 16), 16)
    keep = pltpu.make_async_copy(r_ref.at[core], rg.at[core, row, own], local_sem.at[0])
    keep.start()
    pending = []
    sent = []

    def near(dx, flip):
        k = other if flip else core
        return remote(
            r_ref.at[k], rg.at[k, row, own],
            near_send.at[dx, flip], near_recv.at[(n_x - dx) % n_x, flip], at(dx, k),
        )

    order = [0, 1, n_x - 1, 2]
    for dx in order:
        for flip in range(2):
            if dx == 0 and flip == 0:
                continue
            copy = near(dx, flip)
            copy.start()
            sent.append(copy)
    keep.wait()

    def chunk(block, i):
        start = pl.multiple_of(lax.rem(x + order[i], n_x) * 32, 32)
        return rg.at[core, block, pl.ds(start, 32)]

    def pass_to_mate(block, slot, i):
        copy = remote(
            chunk(block, i), chunk(block, i), pair_send.at[slot, i], pair_recv.at[slot, i], mate
        )
        copy.start()
        sent.append(copy)

    def mate_chunk_wait(slot, i):
        ref = rg.at[other, 0, pl.ds(0, 32)]
        remote(ref, ref, pair_send.at[slot, i], pair_recv.at[slot, i], mate).wait_recv()

    fown = pl.ds(pl.multiple_of(col * 64, 64), 64)
    last = 3
    for step in range(last + 2):
        for i in range(4):
            for way in range(2):
                if step == 0 and way == 1:
                    pass
                block = lax.rem(row + (n_row - step if way == 0 else step), n_row)
                if step == 0:
                    if way == 0:
                        dx = order[i]
                        for flip in range(2):
                            if dx == 0 and flip == 0:
                                continue
                            src = r_ref.at[0]
                            remote(
                                src, src, near_send.at[0, 0], near_recv.at[dx, flip], mate
                            ).wait_recv()
                else:
                    if step == last + 1 and (i < 2) != (way == 0):
                        continue
                    ref = chunk(block, i)
                    remote(
                        ref, ref, ring_send.at[way, step - 1, i], ring_recv.at[way, step - 1, i], mate
                    ).wait_recv()
                if step < last or (step == last and (i < 2) == (way == 0)):
                    copy = remote(
                        chunk(block, i), chunk(block, i),
                        ring_send.at[way, step, i], ring_recv.at[way, step, i],
                        up if way == 0 else down,
                    )
                    copy.start()
                    sent.append(copy)
                if step == 0:
                    if way == 0:
                        pass_to_mate(block, 0, i)
                elif step <= last:
                    pass_to_mate(block, 1 + 2 * (step - 1) + way, i)
                else:
                    pass_to_mate(block, 7, i)
        if step == 0:
            keep_f = pltpu.make_async_copy(f_ref, fg.at[:, fown], local_sem.at[1])
            keep_f.start()
            for dx in (1, n_x - 1, 2):
                copy = remote(
                    f_ref, fg.at[:, fown], wide_send.at[dx],
                    wide_recv.at[(n_x - dx) % n_x], at(dx, core),
                )
                copy.start()
                sent.append(copy)
            copy = remote(f_ref, fg.at[:, fown], mate_send.at[0], mate_recv.at[0], mate)
            copy.start()
            sent.append(copy)
            keep_f.wait()
    for dx in (1, n_x - 1, 2):
        there = pl.ds(pl.multiple_of(lax.rem(x + dx, n_x) * 128 + core * 64, 64), 64)
        ref = fg.at[:, there]
        remote(ref, ref, wide_send.at[dx], wide_recv.at[dx], mate).wait_recv()
        copy = remote(ref, ref, mate_send.at[dx], mate_recv.at[dx], mate)
        copy.start()
        sent.append(copy)
    for dx in range(n_x):
        remote(f_ref, f_ref, mate_send.at[dx], mate_recv.at[dx], mate).wait_recv()
    for slot in range(8):
        for i in range(4):
            mate_chunk_wait(slot, i)
    for copy in sent:
        copy.wait_send()


def gather(r, f, n_row, n_x):
    dma = pltpu.SemaphoreType.DMA
    return pl.pallas_call(
        functools.partial(gather_kernel, n_row, n_x),
        out_shape=(
            jax.ShapeDtypeStruct((2, n_row, 1024 // n_row, 1024), jnp.float32),
            jax.ShapeDtypeStruct((2, 512, 1024), jnp.float32),
        ),
        in_specs=[pl.BlockSpec(memory_space=pltpu.VMEM)] * 2,
        out_specs=[pl.BlockSpec(memory_space=pltpu.VMEM)] * 2,
        scratch_shapes=[
            dma((4, 2)), dma((4, 2)), dma((2, 4, 4)), dma((2, 4, 4)), dma((8, 4)), dma((8, 4)),
            dma((4,)), dma((4,)), dma((4,)), dma((4,)), dma((2,)),
        ],
        compiler_params=pltpu.CompilerParams(
            collective_id=0, has_side_effects=True, vmem_limit_bytes=32 << 20
        ),
    )(r, f)


PARTS = 5


def sum_kernel(a_ref, out, mid, fin, s0, r0, s1, r1, s2, r2, s3, r3):
    pole, row, col = lax.axis_index("pole"), lax.axis_index("row"), lax.axis_index("col")
    nxt, prv, opp = lax.rem(pole + 1, 4), lax.rem(pole + 3, 4), lax.rem(pole + 2, 4)
    to = ((nxt, row, col), (prv, row, col))
    owner = (nxt, prv)
    barrier = pltpu.get_barrier_semaphore()
    for peer in to:
        pl.semaphore_signal(barrier, inc=1, device_id=peer, device_id_type=MESH)
    pl.semaphore_wait(barrier, 2)

    def remote(src, dst, ssem, rsem, dev):
        return pltpu.make_async_remote_copy(
            src_ref=src, dst_ref=dst, send_sem=ssem, recv_sem=rsem,
            device_id=dev, device_id_type=MESH,
        )

    sent = []

    def go(copy):
        copy.start()
        sent.append(copy)

    for t in range(PARTS):
        for w in range(2):
            go(remote(a_ref.at[opp, w, t], mid.at[w, t], s0.at[w, t], r0.at[w, t], to[w]))
    for t in range(PARTS):
        for w in range(2):
            go(remote(a_ref.at[owner[w], 1 - w, t], fin.at[w, 1 - w, t],
                      s1.at[w, 1 - w, t], r1.at[w, 1 - w, t], to[w]))
        for w in range(2):
            ref = mid.at[w, t]
            remote(ref, ref, s0.at[w, t], r0.at[w, t], to[w]).wait_recv()
            mid[w, t] += a_ref[owner[w], w, t]
            go(remote(mid.at[w, t], fin.at[w, w, t], s1.at[w, w, t], r1.at[w, w, t], to[w]))
    for t in range(PARTS):
        for h in range(2):
            for w in range(2):
                ref = fin.at[w, h, t]
                remote(ref, ref, s1.at[w, h, t], r1.at[w, h, t], to[w]).wait_recv()
            out[pole, h, t] = a_ref[pole, h, t] + (fin[0, h, t] + fin[1, h, t])
        for w in range(2):
            for h in (w, 1 - w):
                go(remote(out.at[pole, h, t], out.at[pole, h, t],
                          s2.at[w, h, t], r2.at[w, h, t], to[w]))
    for t in range(PARTS):
        for w in range(2):
            src = prv if w == 0 else nxt
            ref = out.at[src, w, t]
            remote(ref, ref, s2.at[w, w, t], r2.at[w, w, t], to[w]).wait_recv()
            go(remote(ref, ref, s3.at[w, t], r3.at[w, t], to[w]))
    for t in range(PARTS):
        for w in range(2):
            ref = out.at[pole, 1 - w, t]
            remote(ref, ref, s2.at[w, 1 - w, t], r2.at[w, 1 - w, t], to[w]).wait_recv()
            remote(ref, ref, s3.at[w, t], r3.at[w, t], to[w]).wait_recv()
    for copy in sent:
        copy.wait_send()


def pole_sum(a):
    dma = pltpu.SemaphoreType.DMA
    n = a.shape[3]
    return pl.pallas_call(
        sum_kernel,
        out_shape=jax.ShapeDtypeStruct(a.shape, a.dtype),
        in_specs=[pl.BlockSpec(memory_space=pltpu.VMEM)],
        out_specs=pl.BlockSpec(memory_space=pltpu.VMEM),
        scratch_shapes=[
            pltpu.VMEM((2, PARTS, n, 256), jnp.float32),
            pltpu.VMEM((2, 2, PARTS, n, 256), jnp.float32),
            dma((2, PARTS)), dma((2, PARTS)), dma((2, 2, PARTS)), dma((2, 2, PARTS)),
            dma((2, 2, PARTS)), dma((2, 2, PARTS)), dma((2, PARTS)), dma((2, PARTS)),
        ],
        compiler_params=pltpu.CompilerParams(
            collective_id=1, has_side_effects=True, vmem_limit_bytes=32 << 20
        ),
    )(a)


def shards(
    n_row, n_x,
    root_inverse,
    node_factor,
    node_inverse,
    leaf_root_factor,
    leaf_node_factor,
    leaf_inverse,
    leaf_pattern,
    pole_weight,
):
    own_t = jnp.swapaxes(node_factor[:, 0], 1, 2)
    width = own_t.shape[1]
    node_inv = node_inverse[:, 0]
    node_leaf = leaf_node_factor[:, 0]
    leaf_inv = leaf_inverse[:, 0]
    block_rows = leaf_root_factor.shape[2] // leaf_pattern.shape[1]
    row_mask = jnp.repeat(leaf_pattern[0].astype(jnp.float32), block_rows)
    masked = leaf_root_factor[:, 0] * row_mask[None, :, None]
    root, factor_t = gather(root_inverse, own_t, n_row, n_x)
    root = root.reshape(2, 1024, 1024)
    col_index = lax.axis_index("col")
    own_rows = lax.dynamic_slice_in_dim(node_inv, col_index * width, width, 1)
    off = jnp.einsum("pij,pkj->pik", root, factor_t, precision=high)
    off_own = jnp.einsum("pkj,pij->pki", own_t, root, precision=high)
    times = product(root, masked)
    carried = product(off, node_leaf)
    upper = carried - times
    middle = (
        jnp.einsum("pij,pik->pjk", off, masked, precision=high)
        - product(node_inv, node_leaf)
        - product(factor_t, carried)
    )
    diag_rows = own_rows + product(own_t, off)
    lower = (
        leaf_inv
        - jnp.einsum("pij,pik->pjk", masked, upper, precision=high)
        - jnp.einsum("pij,pik->pjk", node_leaf, middle, precision=high)
    )
    terms = (
        weighted(pole_weight, root_inverse),
        weighted(pole_weight, -off_own),
        weighted(pole_weight, diag_rows),
        weighted(pole_weight, upper),
        weighted(pole_weight, middle),
        weighted(pole_weight, lower),
    )
    packed = jnp.concatenate([term.reshape(-1, 256) for term in terms], axis=0)
    total = pole_sum(packed.reshape(4, 2, PARTS, -1, 256)).reshape(-1, 256)
    outs, start = [], 0
    for term in terms:
        rows = term.size // 256
        outs.append(total[start:start + rows].reshape(term.shape))
        start += rows
    return (outs[0], outs[1].T[None], outs[2][None], outs[3][None], outs[4][None], outs[5][None])


def solution(mesh):
    return jax.shard_map(
        functools.partial(shards, mesh.shape["row"], mesh.shape["col"] // 2),
        mesh=mesh,
        in_specs=(
            P("pole", ("row", "col"), None),
            P("pole", "row", None, "col"),
            P("pole", "row", None, None),
            P("pole", ("row", "col"), None, None),
            P("pole", ("row", "col"), None, None),
            P("pole", ("row", "col"), None, None),
            P(("row", "col"), None),
            P("pole"),
        ),
        out_specs=(
            P(("row", "col"), None),
            P("row", None, "col"),
            P("row", "col", None),
            P(("row", "col"), None, None),
            P(("row", "col"), None, None),
            P(("row", "col"), None, None),
        ),
        check_vma=False,
    )
```

time: 272 us -> 159 us (0.58)
  waiting for transfers between devices: 201 us -> 0 us
  Pallas kernels: 0 us -> 98.6 us
  between operations: 13.9 us -> 0.87 us
  local copies, waits for them, and re-layouts: 10.7 us -> 15.7 us
    all_gather x3 -> x0, waiting for transfers between devices: 131 us -> none  [the longest x1 82 us: shards(): lax.all_gather(root_inverse, ('row', 'col'), axis=1, tiled=True)]
    pallas_call x0 -> x2, Pallas kernels: none -> 98.6 us  [the longest x1 55.8 us: gather(): pl.pallas_call(functools.partial(gather_kernel, n_row, n_x), out_shape=(j...]
    psum x1 -> x0, waiting for transfers between devices: 69.4 us -> none  [shards(): lax.psum((upper_levels[0], upper_levels[1], upper_levels[2], leaf_levels[...]
    unnamed x33 -> x37, local copies, waits for them, and re-layouts: 10.6 us -> 9.06 us
    dot_general x7 -> x10, matrix products: 41 us -> 40.9 us  [the longest x5 18.2 us: product(): return jnp.matmul(left, right, precision=high)]
  transfers between devices with their start and end apart: 4 -> 0, of which waited for: 4 -> 0; matrix products, arithmetic and copies ran while one was open for 6% -> 0% of each run, Pallas kernels for 0% -> 0%
where the time goes in v1:
time: 159 us; the launch traced here: 158 us
  Pallas kernels  98.6 us (62%)
  matrix products  40.9 us (26%)
  local copies, waits for them, and re-layouts  15.7 us (10%)
  other arithmetic  1.8 us (1%)
    pallas_call x1, Pallas kernels, gather(): pl.pallas_call(functools.partial(gather_kernel, n_row, n_x), out_shape=(j...  55.8 us
    pallas_call x1, Pallas kernels, pole_sum(): pl.pallas_call(sum_kernel, out_shape=jax.ShapeDtypeStruct(a.shape, a.dtyp...  42.7 us
    dot_general x5, matrix products, product(): return jnp.matmul(left, right, precision=high)  18.2 us
    dot_general x1, matrix products, shards(): off = jnp.einsum('pij,pkj->pik', root, factor_t, precision=high)  10.2 us
    unnamed x37, local copies, waits for them, and re-layouts  9.06 us
    dot_general x1, matrix products, shards(): off_own = jnp.einsum('pkj,pij->pki', own_t, root, precision=high)  3.93 us
    dot_general x1, matrix products, shards(): jnp.einsum('pij,pik->pjk', off, masked, precision=high)  3.79 us
    dot_general x1, matrix products, shards(): jnp.einsum('pij,pik->pjk', masked, upper, precision=high)  3.69 us

profile of v1, /device:TPU:6, one launch (start us, length us, event | category | flops | bytes accessed | tf_op | source)
XLA Modules:
  0.0 157.8 jit_solution(10615069135604111712)
XLA Ops:
  0.7 0.7 convert_bitcast_fusion
  1.5 1.1 multiply_reduce_fusion.2
  2.6 3.6 %fusion = f32[2,512,256]{2,1,0:T(8,128)} fusion(f32[2,1,512,512]{3,2,1,0:T(8,128)} %param.10, f32[2,1,512,256]{3,2,1,0:T(8,128)S(1)} %copy-done), kind=kOutput, calls=%fused_computation | convolution fusion | flops 805306368 | bytes 4194304 | tf_op jit(solution)/shard_map/dot_general | solution.py:15
  6.8 55.8 %shard_map.127 = (f32[2,8,128,1024]{3,2,1,0:T(8,128)S(1)}, f32[2,512,1024]{2,1,0:T(8,128)S(1)}) custom-call(f32[2,16,1024]{2,1,0:T(8,128)S(1)} %copy-done.6, f32[2,64,1024]{2,1,0:T(8,128)S(1)} %bitcast.88), custom_call_target="tpu_custom_call" | custom-call | tf_op jit(solution)/shard_map/pallas_call | solution.py:160
  62.7 1.9 %copy-done.2 = f32[2,512,1024]{2,1,0:T(8,128)} copy-done((f32[2,512,1024]{2,1,0:T(8,128)}, f32[2,512,1024]{2,1,0:T(8,128)S(1)}, u32[]{:S(2)}) %copy-start.2) | copy-done | bytes 4194328
  64.6 3.9 %fusion.12 = f32[1024,64]{0,1:T(8,128)S(1)} fusion(f32[2,1024,1024]{2,1,0:T(8,128)S(1)} %bitcast.78, f32[2,1,1024,64]{2,3,1,0:T(8,128)S(1)} %copy-done.4, f32[2]{0:T(128)S(1)} %copy-done.13), kind=kOutput, calls=%fused_computation.17 | convolution fusion | flops 805634048 | bytes 9175048 | tf_op jit(solution)/shard_map/pkj,pij->pki/dot_general | solution.py:284
  68.6 0.7 constant_dynamic-update-slice_fusion.4
  69.3 10.2 %fusion.25 = f32[2,1024,512]{2,1,0:T(8,128)S(1)} fusion(f32[2,1024,1024]{2,1,0:T(8,128)} %bitcast.79, f32[2,512,1024]{2,1,0:T(8,128)} %copy-done.2), kind=kOutput, calls=%fused_computation.44 | convolution fusion | flops 6442450944 | bytes 16777216 | tf_op jit(solution)/shard_map/pij,pkj->pik/dot_general | solution.py:283
  79.6 3.8 %fusion.6 = f32[2,512,256]{2,1,0:T(8,128)S(1)} fusion(f32[2,512,256]{2,1,0:T(8,128)S(1)} %copy-done.10, f32[2,1024,512]{2,1,0:T(8,128)S(1)} %fusion.25, f32[2,1,1024,256]{3,2,1,0:T(8,128)S(1)} %copy-done.7, f32[1024]{0:T(1024)S(1)} %broadcast_bitcast_fusion), kind=kOutput, calls=%fused_computation.8 | convolution fusion | flops 1611399168 | bytes 8392704 | tf_op jit(solution)/shard_map/pij,pik->pjk/dot_general | solution.py:289
  83.4 2.5 %fusion.15 = f32[64,512]{1,0:T(8,128)S(1)} fusion(f32[2,1024,512]{2,1,0:T(8,128)S(1)} %fusion.25, f32[2,1,1024,64]{2,3,1,0:T(8,128)S(1)} %copy-done.4, f32[2,1,512,512]{3,2,1,0:T(8,128)} %param.10, s32[]{:T(128)S(6)} %select_n.3, f32[2]{0:T(128)S(1)} %copy-done.13), kind=kOutput, calls=%fused_computation.21 | convolution fusion | flops 402817024 | bytes 5111820 | tf_op jit(solution)/shard_map/dot_general | solution.py:15
  85.9 1.9 %fusion.18 = f32[2,1024,256]{2,1,0:T(8,128)S(1)} fusion(f32[2,1024,512]{2,1,0:T(8,128)S(1)} %fusion.25, f32[2,1,512,256]{3,2,1,0:T(8,128)S(1)} %copy-done), kind=kOutput, calls=%fused_computation.25 | convolution fusion | flops 1610612736 | bytes 7340032 | tf_op jit(solution)/shard_map/dot_general | solution.py:15
  87.8 6.2 %multiply_reduce_fusion = (f32[1024,256]{1,0:T(8,128)}, f32[2,1024,256]{2,1,0:T(8,128)}) fusion(f32[2]{0:T(128)S(1)} %copy-done.13, f32[2,1024,256]{2,1,0:T(8,128)S(1)} %fusion.18, f32[2,1024,1024]{2,1,0:T(8,128)S(1)} %bitcast.82, f32[2,1,1024,256]{3,2,1,0:T(8,128)S(1)} %copy-done.7, f32[1024]{0:T(1024)S(1)} %broadcast_bitcast_fusion), kind=kOutput, calls=%fused_computation.3 | convolution fusion | flops 3223060480 | bytes 15732744 | tf_op jit(solution)/shard_map/dot_general | solution.py:15
  94.0 4.1 %multiply_reduce_fusion.1 = (f32[512,256]{1,0:T(8,128)}, f32[2,512,256]{2,1,0:T(8,128)}) fusion(f32[2]{0:T(128)S(1)} %copy-done.13, f32[2,512,256]{2,1,0:T(8,128)S(1)} %fusion.6, f32[2,512,1024]{2,1,0:T(8,128)S(1)} %copy-done.3, f32[2,1024,256]{2,1,0:T(8,128)S(1)} %fusion.18), kind=kOutput, calls=%fused_computation.27 | convolution fusion | flops 1611268096 | bytes 8912904 | tf_op jit(solution)/shard_map/dot_general | solution.py:15
  98.8 2.6 %constant_dynamic-update-slice_fusion.2 = f32[2240,256]{1,0:T(8,128)} fusion(f32[2240,256]{1,0:T(8,128)} %constant_dynamic-update-slice_fusion.3, f32[1024,256]{1,0:T(8,128)} %get-tuple-element.12), kind=kLoop, calls=%fused_computation.38 | loop fusion | bytes 2097152
  101.3 0.8 constant_dynamic-update-slice_fusion.1
  102.2 3.7 %fusion.10 = f32[2,256,256]{2,1,0:T(8,128)S(1)} fusion(f32[2,1024,256]{2,1,0:T(8,128)} %get-tuple-element.13, f32[2,1,1024,256]{3,2,1,0:T(8,128)S(1)} %copy-done.8, f32[1024]{0:T(1024)S(1)} %broadcast_bitcast_fusion, f32[2,1,256,256]{3,2,1,0:T(8,128)S(1)} %copy-done.12), kind=kOutput, calls=%fused_computation.15 | convolution fusion | flops 805961728 | bytes 5246976 | tf_op jit(solution)/shard_map/pij,pik->pjk/dot_general | solution.py:296
  105.9 1.0 fusion.11
  106.9 0.7 constant_dynamic-update-slice_fusion
  107.7 1.6 %copy-done.5 = f32[2240,256]{1,0:T(8,128)S(1)} copy-done((f32[2240,256]{1,0:T(8,128)S(1)}, f32[2240,256]{1,0:T(8,128)}, u32[]{:S(2)}) %copy-start.5) | copy-done | bytes 2293784
  109.3 42.7 %shard_map.128 = f32[4,2,5,56,256]{4,3,2,1,0:T(8,128)S(1)} custom-call(f32[4,2,5,56,256]{4,3,2,1,0:T(8,128)S(1)} %bitcast.89), custom_call_target="tpu_custom_call" | custom-call | tf_op jit(solution)/shard_map/pallas_call | solution.py:243
  153.4 0.8 slice_bitcast_fusion.1
  154.3 0.8 slice_bitcast_fusion.2
  155.1 1.0 slice_bitcast_fusion
  156.1 1.7 %reshape.47 = f32[64,1024]{1,0:T(8,128)} reshape(f32[256,256]{1,0:T(8,128)} %get-tuple-element.11) | data formatting | bytes 524288 | tf_op jit(solution)/shard_map/reshape | solution.py:312
  (41 shorter events, 2.9 us)
Async XLA Ops:
  0.6 1.9 %copy-start = (f32[2,1,512,256]{3,2,1,0:T(8,128)S(1)}, f32[2,1,512,256]{3,2,1,0:T(8,128)}, u32[]{:S(2)}) copy-start(f32[2,1,512,256]{3,2,1,0:T(8,128)} %param.12) | copy-start | bytes 3145732
  1.5 5.3 %copy-start.4 = (f32[2,1,1024,64]{2,3,1,0:T(8,128)S(1)}, f32[2,1,1024,64]{2,3,1,0:T(8,128)}, u32[]{:S(2)}) copy-start(f32[2,1,1024,64]{2,3,1,0:T(8,128)} %param.9) | copy-start | bytes 1572868
  1.5 5.3 %copy-start.6 = (f32[2,16,1024]{2,1,0:T(8,128)S(1)}, f32[2,16,1024]{2,1,0:T(8,128)}, u32[]{:S(2)}) copy-start(f32[2,16,1024]{2,1,0:T(8,128)} %r_ref.1) | copy-start | bytes 393220
  2.6 62.0 %copy-start.13 = (f32[2]{0:T(128)S(1)}, f32[2]{0:T(128)}, u32[]{:S(2)}) copy-start(f32[2]{0:T(128)} %param.15) | copy-start | bytes 28
  62.6 1.9 %copy-start.2 = (f32[2,512,1024]{2,1,0:T(8,128)}, f32[2,512,1024]{2,1,0:T(8,128)S(1)}, u32[]{:S(2)}) copy-start(f32[2,512,1024]{2,1,0:T(8,128)S(1)} %get-tuple-element.9) | copy-start | bytes 12582916
  64.6 3.9 %copy-start.1 = (f32[2,8,128,1024]{3,2,1,0:T(8,128)}, f32[2,8,128,1024]{3,2,1,0:T(8,128)S(1)}, u32[]{:S(2)}) copy-start(f32[2,8,128,1024]{3,2,1,0:T(8,128)S(1)} %get-tuple-element.8) | copy-start | bytes 25165828
  69.3 10.2 %copy-start.7 = (f32[2,1,1024,256]{3,2,1,0:T(8,128)S(1)}, f32[2,1,1024,256]{3,2,1,0:T(8,128)}, u32[]{:S(2)}) copy-start(f32[2,1,1024,256]{3,2,1,0:T(8,128)} %param.11) | copy-start | bytes 6291460
  69.3 10.2 %copy-start.10 = (f32[2,512,256]{2,1,0:T(8,128)S(1)}, f32[2,512,256]{2,1,0:T(8,128)}, u32[]{:S(2)}) copy-start(f32[2,512,256]{2,1,0:T(8,128)} %fusion) | copy-start | bytes 3145732
  79.6 8.2 %slice-start = ((s8[8388608]{0:T(1024)(128)(4,1)}), s8[4194304]{0:T(1024)(128)(4,1)S(1)}, s32[]{:S(2)}) async-start(s8[8388608]{0:T(1024)(128)(4,1)} %bitcast.80), calls=%async_computation | async-start | bytes 8388608
  83.4 4.4 %slice-start.1 = ((s8[8388608]{0:T(1024)(128)(4,1)}), s8[4194304]{0:T(1024)(128)(4,1)S(1)}, s32[]{:S(2)}) async-start(s8[8388608]{0:T(1024)(128)(4,1)} %bitcast.80), calls=%async_computation.1 | async-start | bytes 8388608
  87.8 6.2 %copy-start.3 = (f32[2,512,1024]{2,1,0:T(8,128)S(1)}, f32[2,512,1024]{2,1,0:T(8,128)}, u32[]{:S(2)}) copy-start(f32[2,512,1024]{2,1,0:T(8,128)} %copy-done.2) | copy-start | bytes 12582916
  98.1 4.1 %copy-start.8 = (f32[2,1,1024,256]{3,2,1,0:T(8,128)S(1)}, f32[2,1,1024,256]{3,2,1,0:T(8,128)}, u32[]{:S(2)}) copy-start(f32[2,1,1024,256]{3,2,1,0:T(8,128)} %param.11) | copy-start | bytes 6291460
  98.1 3.3 %copy-start.11 = (f32[512,256]{1,0:T(8,128)S(1)}, f32[512,256]{1,0:T(8,128)}, u32[]{:S(2)}) copy-start(f32[512,256]{1,0:T(8,128)} %get-tuple-element.14) | copy-start | bytes 1572868
  98.1 4.1 %copy-start.12 = (f32[2,1,256,256]{3,2,1,0:T(8,128)S(1)}, f32[2,1,256,256]{3,2,1,0:T(8,128)}, u32[]{:S(2)}) copy-start(f32[2,1,256,256]{3,2,1,0:T(8,128)} %param.13) | copy-start | bytes 1572868
  102.2 3.7 %copy-start.9 = (f32[2,512,256]{2,1,0:T(8,128)S(1)}, f32[2,512,256]{2,1,0:T(8,128)}, u32[]{:S(2)}) copy-start(f32[2,512,256]{2,1,0:T(8,128)} %get-tuple-element.15) | copy-start | bytes 3145732
  107.7 1.6 %copy-start.5 = (f32[2240,256]{1,0:T(8,128)S(1)}, f32[2240,256]{1,0:T(8,128)}, u32[]{:S(2)}) copy-start(f32[2240,256]{1,0:T(8,128)} %constant_dynamic-update-slice_fusion) | copy-start | bytes 6881284

commit v2 on v0

v2 whole, which is shorter than its diff:
```python
import functools

import jax
import jax.numpy as jnp
from jax import lax
from jax.experimental import pallas as pl
from jax.experimental.pallas import tpu as pltpu
from jax.sharding import PartitionSpec as P

MESH = pl.DeviceIdType.MESH
F32, BF16 = jnp.float32, jnp.bfloat16
ROWS, WIDE, LEAF = 1024, 512, 256
Z, X = 8, 4


def split(value):
    hi = value.astype(BF16)
    return hi, (value - hi.astype(F32)).astype(BF16)


def nn(left, right):
    return lax.dot_general(left, right, (((1,), (0,)), ((), ())), preferred_element_type=F32)


def nt(left, right):
    return lax.dot_general(left, right, (((1,), (1,)), ((), ())), preferred_element_type=F32)


def three(dot, stacked, hi, lo):
    half = stacked.shape[0] // 2
    both = dot(stacked, hi)
    return both[:half] + both[half:] + dot(stacked[:half], lo)


class Part:
    def __init__(self, index, shape, mid, fin, src, out):
        self.index, self.shape, self.mid, self.fin, self.src, self.out = index, shape, mid, fin, src, out


def kernel(
    pat, weight, r_ref, f_ref, d_hbm, a_hbm, n_hbm, l_hbm, dw_hbm,
    rb, no, nd, lr, ln, ld,
    dbuf, abuf, nbuf, lbuf, dwbuf,
    rg, fg, ft, fohl, whi, wlo, nhi, nlo, nthl, dn, mt, rhl, ghl,
    ups, offd, offo, diag, rootw, lnw, low,
    mids, fins, omid, ofin, gmid, gfin, rmid, rfin,
    near_send, near_recv, ring_send, ring_recv, pair_send, pair_recv,
    fw_send, fw_recv, fx_send, fx_recv, mate_send, mate_recv, local_sem,
    s0, q0, s1, q1, s2, q2, s3, q3,
):
    pole, row, col = lax.axis_index("pole"), lax.axis_index("row"), lax.axis_index("col")
    x, core = col // 2, lax.rem(col, 2)
    other = 1 - core

    loads = []
    for k, (src, dst) in enumerate(
        ((a_hbm, abuf), (n_hbm, nbuf), (d_hbm, dbuf), (l_hbm, lbuf), (dw_hbm, dwbuf))
    ):
        copy = pltpu.make_async_copy(src, dst, local_sem.at[k])
        copy.start()
        loads.append(copy)

    def at(dx, k):
        return (pole, row, lax.rem(x + dx + X, X) * 2 + k)

    along = ((pole, lax.rem(row + 1, Z), col), (pole, lax.rem(row + Z - 1, Z), col))
    beside = (at(1, core), at(X - 1, core))
    mate = (pole, row, x * 2 + other)
    nxt, prv, opp = lax.rem(pole + 1, 4), lax.rem(pole + 3, 4), lax.rem(pole + 2, 4)
    turn = ((nxt, row, col), (prv, row, col))
    owner = (nxt, prv)

    barrier = pltpu.get_barrier_semaphore()
    peers = [*along, mate, *turn] + [at(dx, k) for dx in range(1, X) for k in range(2)]
    for peer in peers:
        pl.semaphore_signal(barrier, inc=1, device_id=peer, device_id_type=MESH)
    pl.semaphore_wait(barrier, len(peers))

    def remote(src, dst, ssem, rsem, dev):
        return pltpu.make_async_remote_copy(
            src_ref=src, dst_ref=dst, send_sem=ssem, recv_sem=rsem,
            device_id=dev, device_id_type=MESH,
        )

    sent = []

    def go(src, dst, ssem, rsem, dev):
        copy = remote(src, dst, ssem, rsem, dev)
        copy.start()
        sent.append(copy)

    def got(ref, ssem, rsem):
        remote(ref, ref, ssem, rsem, mate).wait_recv()

    own = pl.ds(pl.multiple_of(col * 16, 16), 16)
    for dx in range(X):
        for flip in range(2):
            if dx or flip:
                k = other if flip else core
                go(r_ref.at[k], rg.at[k, row, own], near_send.at[dx, flip],
                   near_recv.at[(X - dx) % X, flip], at(dx, k))
    rg[core, row, own] = r_ref[core]

    def chunk(block, i):
        start = pl.multiple_of(lax.rem(x + i, X) * 32, 32)
        return rg.at[core, block, pl.ds(start, 32)]

    def to_mate(block, slot, i):
        go(chunk(block, i), chunk(block, i), pair_send.at[slot, i], pair_recv.at[slot, i], mate)

    def forward(step, i, way, block):
        if step < 3 or (step == 3 and (i < 2) == (way == 0)):
            go(chunk(block, i), chunk(block, i), ring_send.at[way, step, i],
               ring_recv.at[way, step, i], along[way])

    def block_of(step, way):
        return lax.rem(row + (Z - step if way == 0 else step), Z)

    def event(step, i):
        if step == 0:
            for flip in range(2):
                if i or flip:
                    got(r_ref.at[0], near_send.at[0, 0], near_recv.at[i, flip])
            for way in range(2):
                forward(0, i, way, row)
            to_mate(row, 0, i)
            return
        for way in range(2):
            if step == 4 and (i < 2) != (way == 0):
                continue
            block = block_of(step, way)
            got(chunk(block, i), ring_send.at[way, step - 1, i], ring_recv.at[way, step - 1, i])
            forward(step, i, way, block)
            to_mate(block, 7 if step == 4 else 1 + 2 * (step - 1) + way, i)

    def mate_wait(slot):
        for i in range(4):
            got(rg.at[other, 0, pl.ds(0, 32)], pair_send.at[slot, i], pair_recv.at[slot, i])

    def frows(dx, start=0, size=64):
        first = lax.rem(x + dx, X) * 128 + core * 64 + start
        return pl.ds(pl.multiple_of(first, 32), size)

    def f_start(p):
        here = fg.at[p, frows(0)]
        for way in range(2):
            go(ft.at[p], here, fw_send.at[p, way], fw_recv.at[p, way], beside[way])
        go(ft.at[p], here, mate_send.at[p, 0], mate_recv.at[p, 0], mate)

    def f_relay(p):
        for way, dx in ((0, X - 1), (1, 1)):
            ref = fg.at[p, frows(dx)]
            got(ref, fw_send.at[p, way], fw_recv.at[p, way])
            part = fg.at[p, frows(dx, 32 * way, 32)]
            go(part, part, fx_send.at[p, way], fx_recv.at[p, way], beside[way])
            go(ref, ref, mate_send.at[p, 1 + way], mate_recv.at[p, 1 + way], mate)

    def f_last(p):
        for way in range(2):
            got(fg.at[p, frows(2, 32 * way, 32)], fx_send.at[p, way], fx_recv.at[p, way])
        ref = fg.at[p, frows(2)]
        go(ref, ref, mate_send.at[p, 3], mate_recv.at[p, 3], mate)

    def f_use(p):
        for k in range(4):
            got(ft.at[p], mate_send.at[p, k], mate_recv.at[p, k])

        def body(i, _):
            rows = pl.ds(pl.multiple_of(i * 64, 64), 64)
            whi[p, rows], wlo[p, rows] = split(fg[p, rows])
            return 0

        lax.fori_loop(0, 8, body, 0)

    def prep_f(p):
        t = jnp.transpose(f_ref[p])
        ft[p] = t
        fg[p, frows(0)] = t
        fohl[p, 0:64], fohl[p, 64:128] = split(t)

    def prep_a(p):
        for i in range(8):
            t = jnp.transpose(abuf[p, 128 * i:128 * i + 128] * pat[0, i].astype(F32))
            cols = slice(128 * i, 128 * i + 128)
            whi[p, WIDE:, cols], wlo[p, WIDE:, cols] = split(t)

    def prep_n(p):
        n = nbuf[p]
        nhi[p], nlo[p] = split(n)
        nthl[p, 0:LEAF], nthl[p, LEAF:] = split(jnp.transpose(n))

    def prep_d(p):
        for i in range(2):
            rows = slice(256 * i, 256 * i + 256)
            hi, lo = split(dbuf[p, rows])
            dn[p, rows] = nn(hi, nhi[p]) + nn(lo, nhi[p]) + nn(hi, nlo[p])

    def blocks(t):
        return lax.rem(row + t, Z), lax.rem(row + Z - t - 1, Z)

    def pair_cols(get, t):
        b1, b2 = blocks(t)
        return jnp.concatenate(
            [get(pl.ds(pl.multiple_of(b * 128, 128), 128)) for b in (b1, b2)], axis=1
        )

    def piece(t, p):
        w = weight[p]
        for k, b in enumerate(blocks(t)):
            hi, lo = split(rg[p, b])
            rhl[128 * k:128 * k + 128] = hi
            rhl[256 + 128 * k:384 + 128 * k] = lo
        for n in range(2):
            rows = slice(256 * n, 256 * n + 256)
            g = three(nt, rhl[...], whi[p, rows], wlo[p, rows])
            ghl[0:256, rows], ghl[256:512, rows] = split(g)
        times = three(nt, rhl[...], whi[p, WIDE:], wlo[p, WIDE:])
        o = three(nt, fohl[p], rhl[0:256], rhl[256:512])
        y = three(nn, ghl[...], nhi[p], nlo[p])
        up = y - times
        if p == 0:
            ups[t] = w * up
            offd[t] = -(w * o)
        else:
            ups[t] += w * up
            offd[t] -= w * o
        ath = pair_cols(lambda c: whi[p, WIDE:, c], t)
        atl = pair_cols(lambda c: wlo[p, WIDE:, c], t)
        at2 = jnp.concatenate([ath, atl], axis=0)
        yth, ytl = split(jnp.transpose(y))
        yt2 = jnp.concatenate([yth, ytl], axis=0)
        fth = pair_cols(lambda c: whi[p, :WIDE, c], t)
        ftl = pair_cols(lambda c: wlo[p, :WIDE, c], t)
        m = three(nn, at2, ghl[0:256], ghl[256:512]) - three(nt, yt2, fth, ftl)
        uh, ul = split(up)
        e = w * three(nn, at2, uh, ul)
        fo2 = pair_cols(lambda c: fohl[p, :, c], t)
        g2 = w * three(nn, fo2, ghl[0:256], ghl[256:512])
        if t == 0:
            mt[p] = m
        else:
            mt[p] += m
        low[...] -= e
        diag[...] += g2

    parts = {}

    def add_part(name, index, mid, fin, src, out):
        parts[name] = Part(index, None, mid, fin, src, out)

    def stage0(name):
        part = parts[name]
        n = part.index
        for w in range(2):
            go(part.src(opp, w), part.mid(w), s0.at[n, w], q0.at[n, w], turn[w])
        for w in range(2):
            go(part.src(owner[w], 1 - w), part.fin(w, 1 - w),
               s1.at[n, w, 1 - w], q1.at[n, w, 1 - w], turn[w])

    def stage1(name):
        part = parts[name]
        n = part.index
        for w in range(2):
            ref = part.mid(w)
            got(ref, s0.at[n, w], q0.at[n, w])
            ref[...] += part.src(owner[w], w)[...]
            go(ref, part.fin(w, w), s1.at[n, w, w], q1.at[n, w, w], turn[w])

    def stage2(name):
        part = parts[name]
        n = part.index
        for h in range(2):
            for w in range(2):
                got(part.fin(w, h), s1.at[n, w, h], q1.at[n, w, h])
            ref = part.out(pole, h)
            ref[...] = part.src(pole, h)[...] + (part.fin(0, h)[...] + part.fin(1, h)[...])
        for w in range(2):
            for h in (w, 1 - w):
                ref = part.out(pole, h)
                go(ref, ref, s2.at[n, w, h], q2.at[n, w, h], turn[w])

    def stage3(name):
        part = parts[name]
        n = part.index
        for w in range(2):
            ref = part.out(prv if w == 0 else nxt, w)
            got(ref, s2.at[n, w, w], q2.at[n, w, w])
            go(ref, ref, s3.at[n, w], q3.at[n, w], turn[w])

    def stage4(name):
        part = parts[name]
        n = part.index
        for w in range(2):
            ref = part.out(pole, 1 - w)
            got(ref, s2.at[n, w, 1 - w], q2.at[n, w, 1 - w])
            got(ref, s3.at[n, w], q3.at[n, w])

    def m32(v):
        return pl.ds(pl.multiple_of(v, 32), 32)

    def m8(v):
        return pl.ds(pl.multiple_of(v, 8), 8)

    for t in range(4):
        b1, b2 = blocks(t)

        def lr_out(q, h, b1=b1, b2=b2):
            side = q // 2
            return lr.at[m32((b1 + side * (b2 - b1)) * 128 + lax.rem(q, 2) * 64 + h * 32)]

        add_part("lr%d" % t, t, lambda w, t=t: mids.at[t, w], lambda w, h, t=t: fins.at[t, w, h],
                 lambda q, h, t=t: ups.at[t, m32(q * 64 + h * 32)], lr_out)
    for j in range(2):
        n = 4 + j
        add_part("ln%d" % j, n, lambda w, n=n: mids.at[n, w], lambda w, h, n=n: fins.at[n, w, h],
                 lambda q, h, j=j: lnw.at[m32(j * 256 + q * 64 + h * 32)],
                 lambda q, h, j=j: ln.at[m32(j * 256 + q * 64 + h * 32)])
    add_part("ld", 6, lambda w: mids.at[6, w], lambda w, h: fins.at[6, w, h],
             lambda q, h: low.at[m32(q * 64 + h * 32)], lambda q, h: ld.at[m32(q * 64 + h * 32)])
    for n, ts in ((7, pl.ds(0, 3)), (8, pl.ds(3, 1))):
        add_part("of%d" % n, n, lambda w, ts=ts: omid.at[w, ts], lambda w, h, ts=ts: ofin.at[w, h, ts],
                 lambda q, h, ts=ts: offd.at[ts, m8(q * 16 + h * 8)],
                 lambda q, h, ts=ts: offo.at[ts, m8(q * 16 + h * 8)])
    add_part("nd", 9, lambda w: gmid.at[w], lambda w, h: gfin.at[w, h],
             lambda q, h: diag.at[m8(q * 16 + h * 8)], lambda q, h: nd.at[m8(q * 16 + h * 8)])

    def lanes(q, h):
        return pl.ds(pl.multiple_of(q * 256 + h * 128, 128), 128)

    add_part("rb", 10, lambda w: rmid.at[w], lambda w, h: rfin.at[w, h],
             lambda q, h: rootw.at[:, lanes(q, h)], lambda q, h: rb.at[:, lanes(q, h)])

    def finish(p):
        w = weight[p]
        mid = jnp.transpose(mt[p]) - dn[p]
        if p == 0:
            lnw[...] = w * mid
        else:
            lnw[...] += w * mid
        ghl[:, 0:256], ghl[:, 256:512] = split(mid)

    def finish_low(p):
        low[...] -= weight[p] * three(nn, nthl[p], ghl[:, 0:256], ghl[:, 256:512])

    def offdiag_out(ts):
        for t in ts:
            for k, b in enumerate(blocks(t)):
                no[pl.ds(pl.multiple_of(b * 128, 128), 128)] = jnp.transpose(
                    offo[t, :, 128 * k:128 * k + 128]
                )

    event(0, 0)
    prep_f(0)
    event(0, 1)
    prep_f(1)
    event(0, 2)
    event(0, 3)
    f_start(0)
    rootw[...] = weight[0] * r_ref[0] + weight[1] * r_ref[1]
    stage0("rb")
    loads[0].wait()
    prep_a(0)
    event(1, 0)
    f_start(1)
    prep_a(1)
    event(1, 1)
    f_relay(0)
    loads[1].wait()
    prep_n(0)
    stage1("rb")
    event(1, 2)
    prep_n(1)
    loads[2].wait()
    prep_d(0)
    event(1, 3)
    stage2("rb")
    f_last(0)
    prep_d(1)
    event(2, 0)
    f_relay(1)
    loads[3].wait()
    loads[4].wait()
    low[...] = weight[0] * lbuf[0] + weight[1] * lbuf[1]
    diag[...] = weight[0] * dwbuf[0] + weight[1] * dwbuf[1]
    f_use(0)
    mate_wait(0)
    mate_wait(1)
    piece(0, 0)
    stage3("rb")
    event(2, 1)
    f_last(1)
    event(2, 2)
    f_use(1)
    piece(0, 1)
    stage0("lr0")
    event(2, 3)
    event(3, 0)
    mate_wait(2)
    mate_wait(3)
    piece(1, 0)
    stage1("lr0")
    event(3, 1)
    piece(1, 1)
    stage0("lr1")
    stage2("lr0")
    event(3, 2)
    event(3, 3)
    mate_wait(4)
    mate_wait(5)
    piece(2, 0)
    stage1("lr1")
    stage3("lr0")
    event(4, 0)
    event(4, 2)
    piece(2, 1)
    stage0("lr2")
    stage0("of7")
    stage2("lr1")
    event(4, 1)
    event(4, 3)
    mate_wait(6)
    mate_wait(7)
    piece(3, 0)
    stage1("lr2")
    stage1("of7")
    stage3("lr1")
    piece(3, 1)
    for name in ("lr3", "of8", "nd"):
        stage0(name)
    stage2("lr2")
    stage2("of7")
    finish(0)
    finish_low(0)
    finish(1)
    stage0("ln0")
    stage0("ln1")
    for name in ("lr3", "of8", "nd"):
        stage1(name)
    finish_low(1)
    stage0("ld")
    stage3("lr2")
    stage3("of7")
    for name in ("lr3", "of8", "nd"):
        stage2(name)
    for name in ("ln0", "ln1", "ld"):
        stage1(name)
    for name in ("lr3", "of8", "nd"):
        stage3(name)
    for name in ("ln0", "ln1", "ld"):
        stage2(name)
    stage4("of7")
    offdiag_out(range(3))
    for name in ("ln0", "ln1", "ld"):
        stage3(name)
    stage4("of8")
    offdiag_out(range(3, 4))
    for name in ("rb", "lr0", "lr1", "lr2", "lr3", "nd", "ln0", "ln1", "ld"):
        stage4(name)
    for copy in sent:
        copy.wait_send()


def sweep(pattern, weights, root, factor, node_inv, leaf_root, node_leaf, leaf_inv, own_rows):
    dma = pltpu.SemaphoreType.DMA
    vmem = pltpu.VMEM
    f32 = lambda *shape: vmem(shape, F32)
    bf16 = lambda *shape: vmem(shape, BF16)
    n = 11
    return pl.pallas_call(
        kernel,
        out_shape=tuple(
            jax.ShapeDtypeStruct(shape, F32)
            for shape in ((16, ROWS), (ROWS, 64), (64, WIDE), (ROWS, LEAF), (WIDE, LEAF), (LEAF, LEAF))
        ),
        in_specs=[pl.BlockSpec(memory_space=pltpu.SMEM)] * 2
        + [pl.BlockSpec(memory_space=pltpu.VMEM)] * 2
        + [pl.BlockSpec(memory_space=pl.ANY)] * 5,
        out_specs=[pl.BlockSpec(memory_space=pltpu.VMEM)] * 6,
        scratch_shapes=[
            f32(2, WIDE, WIDE), f32(2, ROWS, LEAF), f32(2, WIDE, LEAF), f32(2, LEAF, LEAF), f32(2, 64, WIDE),
            f32(2, Z, 128, ROWS), f32(2, WIDE, ROWS), f32(2, 64, ROWS), bf16(2, 128, ROWS),
            bf16(2, WIDE + LEAF, ROWS), bf16(2, WIDE + LEAF, ROWS),
            bf16(2, WIDE, LEAF), bf16(2, WIDE, LEAF), bf16(2, 2 * LEAF, WIDE),
            f32(2, WIDE, LEAF), f32(2, LEAF, WIDE), bf16(512, ROWS), bf16(512, WIDE),
            f32(4, 256, LEAF), f32(4, 64, 256), f32(4, 64, 256), f32(64, WIDE), f32(16, ROWS),
            f32(WIDE, LEAF), f32(LEAF, LEAF),
            f32(7, 2, 32, LEAF), f32(7, 2, 2, 32, LEAF), f32(2, 4, 8, 256), f32(2, 2, 4, 8, 256),
            f32(2, 8, WIDE), f32(2, 2, 8, WIDE), f32(2, 16, 128), f32(2, 2, 16, 128),
            dma((4, 2)), dma((4, 2)), dma((2, 4, 4)), dma((2, 4, 4)), dma((8, 4)), dma((8, 4)),
            dma((2, 2)), dma((2, 2)), dma((2, 2)), dma((2, 2)), dma((2, 4)), dma((2, 4)), dma((5,)),
            dma((n, 2)), dma((n, 2)), dma((n, 2, 2)), dma((n, 2, 2)),
            dma((n, 2, 2)), dma((n, 2, 2)), dma((n, 2)), dma((n, 2)),
        ],
        compiler_params=pltpu.CompilerParams(
            collective_id=0, has_side_effects=True, vmem_limit_bytes=58 << 20
        ),
    )(pattern, weights, root, factor, node_inv, leaf_root, node_leaf, leaf_inv, own_rows)


def shards(
    root_inverse,
    node_factor,
    node_inverse,
    leaf_root_factor,
    leaf_node_factor,
    leaf_inverse,
    leaf_pattern,
    pole_weight,
):
    node_inv = node_inverse[:, 0]
    own_rows = lax.dynamic_slice_in_dim(node_inv, lax.axis_index("col") * 64, 64, 1)
    outs = sweep(
        leaf_pattern, pole_weight, root_inverse, node_factor[:, 0], node_inv,
        leaf_root_factor[:, 0], leaf_node_factor[:, 0], leaf_inverse[:, 0], own_rows,
    )
    return (outs[0],) + tuple(out[None] for out in outs[1:])


def solution(mesh):
    return jax.shard_map(
        shards,
        mesh=mesh,
        in_specs=(
            P("pole", ("row", "col"), None),
            P("pole", "row", None, "col"),
            P("pole", "row", None, None),
            P("pole", ("row", "col"), None, None),
            P("pole", ("row", "col"), None, None),
            P("pole", ("row", "col"), None, None),
            P(("row", "col"), None),
            P("pole"),
        ),
        out_specs=(
            P(("row", "col"), None),
            P("row", None, "col"),
            P("row", "col", None),
            P(("row", "col"), None, None),
            P(("row", "col"), None, None),
            P(("row", "col"), None, None),
        ),
        check_vma=False,
    )
```

time: 272 us -> 113 us (0.42)
  waiting for transfers between devices: 201 us -> 0 us
  Pallas kernels: 0 us -> 97.6 us
  matrix products: 41 us -> 0 us
  between operations: 13.9 us -> 0.66 us
  other arithmetic: 4.09 us -> 0 us
    all_gather x3 -> x0, waiting for transfers between devices: 131 us -> none  [the longest x1 82 us: shards(): lax.all_gather(root_inverse, ('row', 'col'), axis=1, tiled=True)]
    pallas_call x0 -> x1, Pallas kernels: none -> 97.6 us  [sweep(): pl.pallas_call(kernel, out_shape=tuple((jax.ShapeDtypeStruct(shape, F32)...]
    psum x1 -> x0, waiting for transfers between devices: 69.4 us -> none  [shards(): lax.psum((upper_levels[0], upper_levels[1], upper_levels[2], leaf_levels[...]
    dot_general x7 -> x0, matrix products: 41 us -> none  [product(): return jnp.matmul(left, right, precision=highest)]
    unnamed x33 -> x11, local copies, waits for them, and re-layouts: 10.6 us -> 11.2 us
  transfers between devices with their start and end apart: 4 -> 0, of which waited for: 4 -> 0; matrix products, arithmetic and copies ran while one was open for 6% -> 0% of each run, Pallas kernels for 0% -> 0%
where the time goes in v2:
time: 113 us; the launch traced here: 111 us
  Pallas kernels  97.6 us (86%)
  local copies, waits for them, and re-layouts  12.8 us (11%)
    pallas_call x1, Pallas kernels, sweep(): pl.pallas_call(kernel, out_shape=tuple((jax.ShapeDtypeStruct(shape, F32)...  97.6 us
    unnamed x11, local copies, waits for them, and re-layouts  11.2 us

profile of v2, /device:TPU:6, one launch (start us, length us, event | category | flops | bytes accessed | tf_op | source)
XLA Modules:
  0.0 111.1 jit_solution(17327071182856871821)
XLA Ops:
  0.6 1.7 %dynamic-slice_bitcast_fusion.dw_hbm = f32[2,64,512]{2,1,0:T(8,128)} fusion(f32[2,1,512,512]{3,2,1,0:T(8,128)} %param.10, s32[]{:T(128)S(6)} %select_n.3), kind=kLoop, calls=%fused_computation | loop fusion | bytes 524292 | tf_op jit(solution)/shard_map/dynamic_slice | solution.py:511
  2.3 2.4 %copy.14 = f32[2,1,1024,64]{3,2,0,1:T(8,128)} copy(f32[2,1,1024,64]{2,3,1,0:T(8,128)} %param.9) | data formatting | bytes 1048576 | tf_op args[1]
  4.7 97.6 %shard_map.127 = (f32[16,1024]{1,0:T(8,128)}, f32[1024,64]{1,0:T(8,128)}, f32[64,512]{1,0:T(8,128)}, f32[1024,256]{1,0:T(8,128)}, f32[512,256]{1,0:T(8,128)}, /*index=5*/f32[256,256]{1,0:T(8,128)}) custom-call(s32[1,8]{1,0:T(1,128)} %pat.1, f32[2]{0:T(128)} %weight.1, f32[2,16,1024]{2,1,0:T(8,128)} %r_ref.1, f32[2,1024,64]{2,1,0:T(8,128)} %bitcast.12, ...), custom_call_target="tpu_custom_call" | custom-call | tf_op jit(solution)/shard_map/pallas_call | solution.py:469
  102.3 0.0 copy-start
  102.3 0.0 copy-start.1
  102.3 2.0 %copy.15 = f32[1,1024,64]{1,2,0:T(8,128)} copy(f32[1,1024,64]{2,1,0:T(8,128)} %bitcast.17) | data formatting | bytes 524288
  104.3 1.5 %copy.21 = f32[16,1024]{1,0:T(8,128)} copy(f32[16,1024]{1,0:T(8,128)} %get-tuple-element.30) | data formatting | bytes 131072
  105.8 1.6 %copy.22 = f32[1,64,512]{2,1,0:T(8,128)} copy(f32[1,64,512]{2,1,0:T(8,128)} %bitcast.21) | data formatting | bytes 262144
  107.4 2.3 %copy.23 = f32[1,1024,256]{2,1,0:T(8,128)} copy(f32[1,1024,256]{2,1,0:T(8,128)} %bitcast.15) | data formatting | bytes 2097152
  109.6 0.0 copy-done
  109.6 0.8 copy.24
  110.4 0.0 copy-done.1
  110.4 0.7 copy.25
Async XLA Ops:
  102.3 7.3 %copy-start = (f32[512,256]{1,0:T(8,128)S(1)}, f32[512,256]{1,0:T(8,128)}, u32[]{:S(2)}) copy-start(f32[512,256]{1,0:T(8,128)} %get-tuple-element.16) | copy-start | bytes 1572868
  102.3 8.1 %copy-start.1 = (f32[256,256]{1,0:T(8,128)S(1)}, f32[256,256]{1,0:T(8,128)}, u32[]{:S(2)}) copy-start(f32[256,256]{1,0:T(8,128)} %get-tuple-element.17) | copy-start | bytes 786436

commit v3 on v2

--- a/solution.py
+++ b/solution.py
@@ -38,14 +38,14 @@
 
 
 def kernel(
-    pat, weight, r_ref, f_ref, d_hbm, a_hbm, n_hbm, l_hbm, dw_hbm,
+    pat, weight, r_ref, ft, d_hbm, a_hbm, n_hbm, l_hbm,
     rb, no, nd, lr, ln, ld,
-    dbuf, abuf, nbuf, lbuf, dwbuf,
-    rg, fg, ft, fohl, whi, wlo, nhi, nlo, nthl, dn, mt, rhl, ghl,
+    dbuf, abuf, nbuf, lbuf,
+    rg, fg, fohl, whi, wlo, nhi, nlo, nthl, dn, mt, rhl, ghl,
     ups, offd, offo, diag, rootw, lnw, low,
     mids, fins, omid, ofin, gmid, gfin, rmid, rfin,
     near_send, near_recv, ring_send, ring_recv, pair_send, pair_recv,
-    fw_send, fw_recv, fx_send, fx_recv, mate_send, mate_recv, local_sem,
+    cross_send, cross_recv, fw_send, fw_recv, fx_send, fx_recv, mate_send, mate_recv, local_sem,
     s0, q0, s1, q1, s2, q2, s3, q3,
 ):
     pole, row, col = lax.axis_index("pole"), lax.axis_index("row"), lax.axis_index("col")
@@ -54,7 +54,7 @@
 
     loads = []
     for k, (src, dst) in enumerate(
-        ((a_hbm, abuf), (n_hbm, nbuf), (d_hbm, dbuf), (l_hbm, lbuf), (dw_hbm, dwbuf))
+        ((a_hbm, abuf), (n_hbm, nbuf), (d_hbm, dbuf), (l_hbm, lbuf))
     ):
         copy = pltpu.make_async_copy(src, dst, local_sem.at[k])
         copy.start()
@@ -109,7 +109,7 @@
         go(chunk(block, i), chunk(block, i), pair_send.at[slot, i], pair_recv.at[slot, i], mate)
 
     def forward(step, i, way, block):
-        if step < 3 or (step == 3 and (i < 2) == (way == 0)):
+        if step < 2 or (step == 2 and i < 2) or (step == 3 and i == way):
             go(chunk(block, i), chunk(block, i), ring_send.at[way, step, i],
                ring_recv.at[way, step, i], along[way])
 
@@ -126,12 +126,23 @@
             to_mate(row, 0, i)
             return
         for way in range(2):
-            if step == 4 and (i < 2) != (way == 0):
+            if step == 4 and i != way:
                 continue
             block = block_of(step, way)
+            slot = 7 if step == 4 else 1 + 2 * (step - 1) + way
             got(chunk(block, i), ring_send.at[way, step - 1, i], ring_recv.at[way, step - 1, i])
             forward(step, i, way, block)
-            to_mate(block, 7 if step == 4 else 1 + 2 * (step - 1) + way, i)
+            if step > 2:
+                go(chunk(block, i), chunk(block, i), cross_send.at[slot - 5, i],
+                   cross_recv.at[slot - 5, i], beside[i])
+            to_mate(block, slot, i)
+
+    def cross(slot):
+        block = block_of(4 if slot == 7 else 3, (slot - 5) % 2)
+        for i in range(2):
+            ref = chunk(block, 3 - i)
+            got(ref, cross_send.at[slot - 5, i], cross_recv.at[slot - 5, i])
+            to_mate(block, slot, 3 - i)
 
     def mate_wait(slot):
         for i in range(4):
@@ -173,8 +184,7 @@
         lax.fori_loop(0, 8, body, 0)
 
     def prep_f(p):
-        t = jnp.transpose(f_ref[p])
-        ft[p] = t
+        t = ft[p]
         fg[p, frows(0)] = t
         fohl[p, 0:64], fohl[p, 64:128] = split(t)
 
@@ -196,34 +206,38 @@
             dn[p, rows] = nn(hi, nhi[p]) + nn(lo, nhi[p]) + nn(hi, nlo[p])
 
     def blocks(t):
-        return lax.rem(row + t, Z), lax.rem(row + Z - t - 1, Z)
+        first = lax.rem(row + t, Z)
+        return [first] if t > 2 else [first, lax.rem(row + Z - t - 1, Z)]
+
+    FIRST = (0, 256, 512, 768, 896)
 
     def pair_cols(get, t):
-        b1, b2 = blocks(t)
-        return jnp.concatenate(
-            [get(pl.ds(pl.multiple_of(b * 128, 128), 128)) for b in (b1, b2)], axis=1
-        )
+        cols = [get(pl.ds(pl.multiple_of(b * 128, 128), 128)) for b in blocks(t)]
+        return cols[0] if len(cols) == 1 else jnp.concatenate(cols, axis=1)
 
     def piece(t, p):
         w = weight[p]
+        size = 128 * len(blocks(t))
+        here = slice(FIRST[t], FIRST[t] + size)
+        top, all_rows = slice(0, size), slice(0, 2 * size)
         for k, b in enumerate(blocks(t)):
             hi, lo = split(rg[p, b])
             rhl[128 * k:128 * k + 128] = hi
-            rhl[256 + 128 * k:384 + 128 * k] = lo
+            rhl[size + 128 * k:size + 128 * k + 128] = lo
         for n in range(2):
             rows = slice(256 * n, 256 * n + 256)
-            g = three(nt, rhl[...], whi[p, rows], wlo[p, rows])
-            ghl[0:256, rows], ghl[256:512, rows] = split(g)
-        times = three(nt, rhl[...], whi[p, WIDE:], wlo[p, WIDE:])
-        o = three(nt, fohl[p], rhl[0:256], rhl[256:512])
-        y = three(nn, ghl[...], nhi[p], nlo[p])
+            g = three(nt, rhl[all_rows], whi[p, rows], wlo[p, rows])
+            ghl[top, rows], ghl[size:2 * size, rows] = split(g)
+        times = three(nt, rhl[all_rows], whi[p, WIDE:], wlo[p, WIDE:])
+        y = three(nn, ghl[all_rows], nhi[p], nlo[p])
         up = y - times
+        o = three(nt, fohl[p], rhl[top], rhl[size:2 * size])
         if p == 0:
-            ups[t] = w * up
-            offd[t] = -(w * o)
+            ups[here] = w * up
+            offd[:, here] = -(w * o)
         else:
-            ups[t] += w * up
-            offd[t] -= w * o
+            ups[here] += w * up
+            offd[:, here] -= w * o
         ath = pair_cols(lambda c: whi[p, WIDE:, c], t)
         atl = pair_cols(lambda c: wlo[p, WIDE:, c], t)
         at2 = jnp.concatenate([ath, atl], axis=0)
@@ -231,11 +245,11 @@
         yt2 = jnp.concatenate([yth, ytl], axis=0)
         fth = pair_cols(lambda c: whi[p, :WIDE, c], t)
         ftl = pair_cols(lambda c: wlo[p, :WIDE, c], t)
-        m = three(nn, at2, ghl[0:256], ghl[256:512]) - three(nt, yt2, fth, ftl)
+        m = three(nn, at2, ghl[top], ghl[size:2 * size]) - three(nt, yt2, fth, ftl)
         uh, ul = split(up)
         e = w * three(nn, at2, uh, ul)
         fo2 = pair_cols(lambda c: fohl[p, :, c], t)
-        g2 = w * three(nn, fo2, ghl[0:256], ghl[256:512])
+        g2 = w * three(nn, fo2, ghl[top], ghl[size:2 * size])
         if t == 0:
             mt[p] = m
         else:
@@ -301,33 +315,46 @@
     def m8(v):
         return pl.ds(pl.multiple_of(v, 8), 8)
 
-    for t in range(4):
+    def m16(v):
+        return pl.ds(pl.multiple_of(v, 16), 16)
+
+    def add_rows(name, n, src, out, small=False):
+        if small:
+            add_part(name, n, lambda w: mids.at[n, w, pl.ds(0, 16)],
+                     lambda w, h: fins.at[n, w, h, pl.ds(0, 16)], src, out)
+        else:
+            add_part(name, n, lambda w: mids.at[n, w], lambda w, h: fins.at[n, w, h], src, out)
+
+    for t in range(3):
         b1, b2 = blocks(t)
 
         def lr_out(q, h, b1=b1, b2=b2):
             side = q // 2
             return lr.at[m32((b1 + side * (b2 - b1)) * 128 + lax.rem(q, 2) * 64 + h * 32)]
 
-        add_part("lr%d" % t, t, lambda w, t=t: mids.at[t, w], lambda w, h, t=t: fins.at[t, w, h],
-                 lambda q, h, t=t: ups.at[t, m32(q * 64 + h * 32)], lr_out)
+        add_rows("lr%d" % t, t, lambda q, h, t=t: ups.at[m32(FIRST[t] + q * 64 + h * 32)], lr_out)
+    for t in (3, 4):
+        b1 = blocks(t)[0]
+        add_rows("lr%d" % t, t, lambda q, h, t=t: ups.at[m16(FIRST[t] + q * 32 + h * 16)],
+                 lambda q, h, b1=b1: lr.at[m16(b1 * 128 + q * 32 + h * 16)], True)
     for j in range(2):
-        n = 4 + j
-        add_part("ln%d" % j, n, lambda w, n=n: mids.at[n, w], lambda w, h, n=n: fins.at[n, w, h],
+        add_rows("ln%d" % j, 5 + j,
                  lambda q, h, j=j: lnw.at[m32(j * 256 + q * 64 + h * 32)],
                  lambda q, h, j=j: ln.at[m32(j * 256 + q * 64 + h * 32)])
-    add_part("ld", 6, lambda w: mids.at[6, w], lambda w, h: fins.at[6, w, h],
-             lambda q, h: low.at[m32(q * 64 + h * 32)], lambda q, h: ld.at[m32(q * 64 + h * 32)])
-    for n, ts in ((7, pl.ds(0, 3)), (8, pl.ds(3, 1))):
-        add_part("of%d" % n, n, lambda w, ts=ts: omid.at[w, ts], lambda w, h, ts=ts: ofin.at[w, h, ts],
-                 lambda q, h, ts=ts: offd.at[ts, m8(q * 16 + h * 8)],
-                 lambda q, h, ts=ts: offo.at[ts, m8(q * 16 + h * 8)])
-    add_part("nd", 9, lambda w: gmid.at[w], lambda w, h: gfin.at[w, h],
+    add_rows("ld", 7, lambda q, h: low.at[m32(q * 64 + h * 32)],
+             lambda q, h: ld.at[m32(q * 64 + h * 32)])
+    for n, ts in ((8, slice(0, 768)), (9, slice(768, 1024))):
+        add_part("of%d" % n, n, lambda w, ts=ts: omid.at[w, :, ts],
+                 lambda w, h, ts=ts: ofin.at[w, h, :, ts],
+                 lambda q, h, ts=ts: offd.at[m8(q * 16 + h * 8), ts],
+                 lambda q, h, ts=ts: offo.at[m8(q * 16 + h * 8), ts])
+    add_part("nd", 10, lambda w: gmid.at[w], lambda w, h: gfin.at[w, h],
              lambda q, h: diag.at[m8(q * 16 + h * 8)], lambda q, h: nd.at[m8(q * 16 + h * 8)])
 
     def lanes(q, h):
         return pl.ds(pl.multiple_of(q * 256 + h * 128, 128), 128)
 
-    add_part("rb", 10, lambda w: rmid.at[w], lambda w, h: rfin.at[w, h],
+    add_part("rb", 11, lambda w: rmid.at[w], lambda w, h: rfin.at[w, h],
              lambda q, h: rootw.at[:, lanes(q, h)], lambda q, h: rb.at[:, lanes(q, h)])
 
     def finish(p):
@@ -345,19 +372,22 @@
     def offdiag_out(ts):
         for t in ts:
             for k, b in enumerate(blocks(t)):
-                no[pl.ds(pl.multiple_of(b * 128, 128), 128)] = jnp.transpose(
-                    offo[t, :, 128 * k:128 * k + 128]
-                )
+                start = FIRST[t] + 128 * k
+                no[:, pl.ds(pl.multiple_of(b * 128, 128), 128)] = offo[:, start:start + 128]
+
+    def all_of(stage, *names):
+        for name in names:
+            stage(name)
 
     event(0, 0)
-    prep_f(0)
     event(0, 1)
-    prep_f(1)
+    f_start(0)
     event(0, 2)
     event(0, 3)
-    f_start(0)
     rootw[...] = weight[0] * r_ref[0] + weight[1] * r_ref[1]
     stage0("rb")
+    prep_f(0)
+    prep_f(1)
     loads[0].wait()
     prep_a(0)
     event(1, 0)
@@ -376,12 +406,12 @@
     stage2("rb")
     f_last(0)
     prep_d(1)
+    loads[3].wait()
+    low[...] = weight[0] * lbuf[0] + weight[1] * lbuf[1]
+    own_rows = pl.ds(pl.multiple_of(col * 64, 64), 64)
+    diag[...] = weight[0] * dbuf[0, own_rows] + weight[1] * dbuf[1, own_rows]
     event(2, 0)
     f_relay(1)
-    loads[3].wait()
-    loads[4].wait()
-    low[...] = weight[0] * lbuf[0] + weight[1] * lbuf[1]
-    diag[...] = weight[0] * dwbuf[0] + weight[1] * dwbuf[1]
     f_use(0)
     mate_wait(0)
     mate_wait(1)
@@ -391,110 +421,123 @@
     f_last(1)
     event(2, 2)
     f_use(1)
+    event(2, 3)
     piece(0, 1)
     stage0("lr0")
-    event(2, 3)
     event(3, 0)
+    event(3, 1)
     mate_wait(2)
     mate_wait(3)
     piece(1, 0)
     stage1("lr0")
-    event(3, 1)
+    event(4, 0)
+    event(4, 1)
+    cross(5)
+    cross(6)
     piece(1, 1)
     stage0("lr1")
     stage2("lr0")
-    event(3, 2)
-    event(3, 3)
+    cross(7)
     mate_wait(4)
     mate_wait(5)
     piece(2, 0)
     stage1("lr1")
     stage3("lr0")
-    event(4, 0)
-    event(4, 2)
     piece(2, 1)
-    stage0("lr2")
-    stage0("of7")
+    all_of(stage0, "lr2", "of8")
     stage2("lr1")
-    event(4, 1)
-    event(4, 3)
     mate_wait(6)
+    piece(3, 0)
+    all_of(stage1, "lr2", "of8")
+    piece(3, 1)
+    stage0("lr3")
+    stage3("lr1")
     mate_wait(7)
-    piece(3, 0)
-    stage1("lr2")
-    stage1("of7")
-    stage3("lr1")
-    piece(3, 1)
-    for name in ("lr3", "of8", "nd"):
-        stage0(name)
-    stage2("lr2")
-    stage2("of7")
+    piece(4, 0)
+    all_of(stage2, "lr2", "of8")
+    stage1("lr3")
+    piece(4, 1)
+    all_of(stage0, "lr4", "nd", "of9")
     finish(0)
+    stage2("lr3")
     finish_low(0)
     finish(1)
-    stage0("ln0")
-    stage0("ln1")
-    for name in ("lr3", "of8", "nd"):
-        stage1(name)
+    all_of(stage0, "ln0", "ln1")
+    all_of(stage3, "lr2", "of8")
+    all_of(stage1, "lr4", "nd", "of9")
     finish_low(1)
     stage0("ld")
-    stage3("lr2")
-    stage3("of7")
-    for name in ("lr3", "of8", "nd"):
-        stage2(name)
-    for name in ("ln0", "ln1", "ld"):
-        stage1(name)
-    for name in ("lr3", "of8", "nd"):
-        stage3(name)
-    for name in ("ln0", "ln1", "ld"):
-        stage2(name)
-    stage4("of7")
+    stage3("lr3")
+    all_of(stage1, "ln0")
+    all_of(stage2, "lr4", "nd", "of9")
+    all_of(stage1, "ln1", "ld")
+    all_of(stage3, "lr4", "nd", "of9")
+    all_of(stage2, "ln0", "ln1", "ld")
+    stage4("of8")
     offdiag_out(range(3))
-    for name in ("ln0", "ln1", "ld"):
-        stage3(name)
-    stage4("of8")
-    offdiag_out(range(3, 4))
-    for name in ("rb", "lr0", "lr1", "lr2", "lr3", "nd", "ln0", "ln1", "ld"):
-        stage4(name)
+    all_of(stage3, "ln0", "ln1", "ld")
+    stage4("of9")
+    offdiag_out(range(3, 5))
+    all_of(stage4, "rb", "lr0", "lr1", "lr2", "lr3", "lr4", "nd", "ln0", "ln1", "ld")
     for copy in sent:
         copy.wait_send()
 
 
-def sweep(pattern, weights, root, factor, node_inv, leaf_root, node_leaf, leaf_inv, own_rows):
+SHAPES = ((16, ROWS), (64, ROWS), (64, WIDE), (ROWS, LEAF), (WIDE, LEAF), (LEAF, LEAF))
+
+
+def sweep(pattern, weights, root, factor, node_inv, leaf_root, node_leaf, leaf_inv):
     dma = pltpu.SemaphoreType.DMA
     vmem = pltpu.VMEM
     f32 = lambda *shape: vmem(shape, F32)
     bf16 = lambda *shape: vmem(shape, BF16)
-    n = 11
+    n = 12
     return pl.pallas_call(
         kernel,
-        out_shape=tuple(
-            jax.ShapeDtypeStruct(shape, F32)
-            for shape in ((16, ROWS), (ROWS, 64), (64, WIDE), (ROWS, LEAF), (WIDE, LEAF), (LEAF, LEAF))
-        ),
+        out_shape=tuple(jax.ShapeDtypeStruct(shape, F32) for shape in SHAPES),
         in_specs=[pl.BlockSpec(memory_space=pltpu.SMEM)] * 2
         + [pl.BlockSpec(memory_space=pltpu.VMEM)] * 2
-        + [pl.BlockSpec(memory_space=pl.ANY)] * 5,
+        + [pl.BlockSpec(memory_space=pl.ANY)] * 4,
         out_specs=[pl.BlockSpec(memory_space=pltpu.VMEM)] * 6,
         scratch_shapes=[
-            f32(2, WIDE, WIDE), f32(2, ROWS, LEAF), f32(2, WIDE, LEAF), f32(2, LEAF, LEAF), f32(2, 64, WIDE),
-            f32(2, Z, 128, ROWS), f32(2, WIDE, ROWS), f32(2, 64, ROWS), bf16(2, 128, ROWS),
+            f32(2, WIDE, WIDE), f32(2, ROWS, LEAF), f32(2, WIDE, LEAF), f32(2, LEAF, LEAF),
+            f32(2, Z, 128, ROWS), f32(2, WIDE, ROWS), bf16(2, 128, ROWS),
             bf16(2, WIDE + LEAF, ROWS), bf16(2, WIDE + LEAF, ROWS),
             bf16(2, WIDE, LEAF), bf16(2, WIDE, LEAF), bf16(2, 2 * LEAF, WIDE),
             f32(2, WIDE, LEAF), f32(2, LEAF, WIDE), bf16(512, ROWS), bf16(512, WIDE),
-            f32(4, 256, LEAF), f32(4, 64, 256), f32(4, 64, 256), f32(64, WIDE), f32(16, ROWS),
+            f32(ROWS, LEAF), f32(64, ROWS), f32(64, ROWS), f32(64, WIDE), f32(16, ROWS),
             f32(WIDE, LEAF), f32(LEAF, LEAF),
-            f32(7, 2, 32, LEAF), f32(7, 2, 2, 32, LEAF), f32(2, 4, 8, 256), f32(2, 2, 4, 8, 256),
+            f32(8, 2, 32, LEAF), f32(8, 2, 2, 32, LEAF), f32(2, 8, ROWS), f32(2, 2, 8, ROWS),
             f32(2, 8, WIDE), f32(2, 2, 8, WIDE), f32(2, 16, 128), f32(2, 2, 16, 128),
             dma((4, 2)), dma((4, 2)), dma((2, 4, 4)), dma((2, 4, 4)), dma((8, 4)), dma((8, 4)),
-            dma((2, 2)), dma((2, 2)), dma((2, 2)), dma((2, 2)), dma((2, 4)), dma((2, 4)), dma((5,)),
+            dma((3, 2)), dma((3, 2)),
+            dma((2, 2)), dma((2, 2)), dma((2, 2)), dma((2, 2)), dma((2, 4)), dma((2, 4)), dma((4,)),
             dma((n, 2)), dma((n, 2)), dma((n, 2, 2)), dma((n, 2, 2)),
             dma((n, 2, 2)), dma((n, 2, 2)), dma((n, 2)), dma((n, 2)),
         ],
         compiler_params=pltpu.CompilerParams(
-            collective_id=0, has_side_effects=True, vmem_limit_bytes=58 << 20
+            collective_id=0, has_side_effects=True, vmem_limit_bytes=56 << 20
         ),
-    )(pattern, weights, root, factor, node_inv, leaf_root, node_leaf, leaf_inv, own_rows)
+    )(pattern, weights, root, factor, node_inv, leaf_root, node_leaf, leaf_inv)
+
+
+def settle_kernel(*refs):
+    ins, outs, sems = refs[:6], refs[6:12], refs[12]
+    copies = [pltpu.make_async_copy(a, b, sems.at[k]) for k, (a, b) in enumerate(zip(ins, outs))]
+    for copy in copies:
+        copy.start()
+    for copy in copies:
+        copy.wait()
+
+
+def settle(arrays):
+    return pl.pallas_call(
+        settle_kernel,
+        out_shape=tuple(jax.ShapeDtypeStruct(shape, F32) for shape in SHAPES),
+        in_specs=[pl.BlockSpec(memory_space=pl.ANY)] * 6,
+        out_specs=[pl.BlockSpec(memory_space=pl.ANY)] * 6,
+        scratch_shapes=[pltpu.SemaphoreType.DMA((6,))],
+    )(*arrays)
 
 
 def shards(
@@ -507,13 +550,11 @@
     leaf_pattern,
     pole_weight,
 ):
-    node_inv = node_inverse[:, 0]
-    own_rows = lax.dynamic_slice_in_dim(node_inv, lax.axis_index("col") * 64, 64, 1)
-    outs = sweep(
-        leaf_pattern, pole_weight, root_inverse, node_factor[:, 0], node_inv,
-        leaf_root_factor[:, 0], leaf_node_factor[:, 0], leaf_inverse[:, 0], own_rows,
-    )
-    return (outs[0],) + tuple(out[None] for out in outs[1:])
+    outs = settle(sweep(
+        leaf_pattern, pole_weight, root_inverse, jnp.swapaxes(node_factor[:, 0], 1, 2),
+        node_inverse[:, 0], leaf_root_factor[:, 0], leaf_node_factor[:, 0], leaf_inverse[:, 0],
+    ))
+    return (outs[0], outs[1].T[None]) + tuple(out[None] for out in outs[2:])
 
 
 def solution(mesh):

time: 113 us -> 175 us (1.55)
  Pallas kernels: 97.6 us -> 173 us
  local copies, waits for them, and re-layouts: 12.8 us -> 0 us
    pallas_call x0 -> x1, Pallas kernels: none -> 70.6 us  [settle(): pl.pallas_call(settle_kernel, out_shape=tuple((jax.ShapeDtypeStruct(shape...]
    unnamed x11 -> x0, local copies, waits for them, and re-layouts: 11.2 us -> none
    pallas_call x1, Pallas kernels: 97.6 us -> 103 us  [sweep(): pl.pallas_call(kernel, out_shape=tuple((jax.ShapeDtypeStruct(shape, F32)...]
where the time goes in v3:
time: 175 us; the launch traced here: 174 us
  Pallas kernels  173 us (99%)
    pallas_call x1, Pallas kernels, sweep(): pl.pallas_call(kernel, out_shape=tuple((jax.ShapeDtypeStruct(shape, F32)...  103 us
    pallas_call x1, Pallas kernels, settle(): pl.pallas_call(settle_kernel, out_shape=tuple((jax.ShapeDtypeStruct(shape...  70.6 us

profile of v3, /device:TPU:6, one launch (start us, length us, event | category | flops | bytes accessed | tf_op | source)
XLA Modules:
  0.0 174.3 jit_solution(15246260893056977072)
XLA Ops:
  0.6 102.8 %shard_map.127 = (f32[16,1024]{1,0:T(8,128)}, f32[64,1024]{1,0:T(8,128)}, f32[64,512]{1,0:T(8,128)}, f32[1024,256]{1,0:T(8,128)}, f32[512,256]{1,0:T(8,128)}, /*index=5*/f32[256,256]{1,0:T(8,128)}) custom-call(s32[1,8]{1,0:T(1,128)} %pat.1, f32[2]{0:T(128)} %weight.1, f32[2,16,1024]{2,1,0:T(8,128)} %r_ref.1, f32[2,64,1024]{2,1,0:T(8,128)} %bitcast.17, ...), custom_call_target="tpu_custom_call" | custom-call | tf_op jit(solution)/shard_map/pallas_call | solution.py:495
  103.4 70.6 %shard_map.128 = (f32[16,1024]{1,0:T(8,128)}, f32[64,1024]{1,0:T(8,128)}, f32[64,512]{1,0:T(8,128)}, f32[1024,256]{1,0:T(8,128)}, f32[512,256]{1,0:T(8,128)}, /*index=5*/f32[256,256]{1,0:T(8,128)}) custom-call(f32[16,1024]{1,0:T(8,128)} %get-tuple-element.18.refs_0_, f32[64,1024]{1,0:T(8,128)} %get-tuple-element.19.refs_1_, ...), custom_call_target="tpu_custom_call" | custom-call | tf_op jit(solution)/shard_map/pallas_call | solution.py:534

commit v4 on v3

--- a/solution.py
+++ b/solution.py
@@ -41,7 +41,7 @@
     pat, weight, r_ref, ft, d_hbm, a_hbm, n_hbm, l_hbm,
     rb, no, nd, lr, ln, ld,
     dbuf, abuf, nbuf, lbuf,
-    rg, fg, fohl, whi, wlo, nhi, nlo, nthl, dn, mt, rhl, ghl,
+    rg, fg, fhi, flo, af, qhi, qlo, nhi, nlo, nthl, dn, rs, xs, vt, vhl, mhl,
     ups, offd, offo, diag, rootw, lnw, low,
     mids, fins, omid, ofin, gmid, gfin, rmid, rfin,
     near_send, near_recv, ring_send, ring_recv, pair_send, pair_recv,
@@ -178,7 +178,7 @@
 
         def body(i, _):
             rows = pl.ds(pl.multiple_of(i * 64, 64), 64)
-            whi[p, rows], wlo[p, rows] = split(fg[p, rows])
+            fhi[p, rows], flo[p, rows] = split(fg[p, rows])
             return 0
 
         lax.fori_loop(0, 8, body, 0)
@@ -186,13 +186,13 @@
     def prep_f(p):
         t = ft[p]
         fg[p, frows(0)] = t
-        fohl[p, 0:64], fohl[p, 64:128] = split(t)
+        af[p, 256:320], af[p, 576:640] = split(t)
 
     def prep_a(p):
         for i in range(8):
             t = jnp.transpose(abuf[p, 128 * i:128 * i + 128] * pat[0, i].astype(F32))
             cols = slice(128 * i, 128 * i + 128)
-            whi[p, WIDE:, cols], wlo[p, WIDE:, cols] = split(t)
+            af[p, 0:256, cols], af[p, 320:576, cols] = split(t)
 
     def prep_n(p):
         n = nbuf[p]
@@ -207,55 +207,72 @@
 
     def blocks(t):
         first = lax.rem(row + t, Z)
-        return [first] if t > 2 else [first, lax.rem(row + Z - t - 1, Z)]
-
-    FIRST = (0, 256, 512, 768, 896)
+        return [first] if t in (0, 4) else [first, lax.rem(row + Z - t, Z)]
+
+    FIRST = (0, 128, 384, 640, 896)
+
+    def span(t):
+        size = 128 * len(blocks(t))
+        start = 2 * FIRST[t]
+        return size, slice(start, start + size), slice(start + size, start + 2 * size), slice(start, start + 2 * size)
+
+    def lane(b):
+        return pl.ds(pl.multiple_of(b * 128, 128), 128)
 
     def pair_cols(get, t):
-        cols = [get(pl.ds(pl.multiple_of(b * 128, 128), 128)) for b in blocks(t)]
+        cols = [get(lane(b)) for b in blocks(t)]
         return cols[0] if len(cols) == 1 else jnp.concatenate(cols, axis=1)
 
-    def piece(t, p):
+    def early(t, p):
+        size, hi_rows, lo_rows, all_rows = span(t)
+        here = slice(FIRST[t], FIRST[t] + size)
+        for k, b in enumerate(blocks(t)):
+            start = 2 * FIRST[t] + 128 * k
+            rs[p, start:start + 128], rs[p, start + size:start + size + 128] = split(rg[p, b])
+        xs[p, here] = three(nt, rs[p, all_rows], af[p, 0:256], af[p, 320:576])
+        fo = jnp.concatenate([af[p, 256:320], af[p, 576:640]], axis=0)
+        o = weight[p] * three(nt, fo, rs[p, hi_rows], rs[p, lo_rows])
+        if p == 0:
+            offd[:, here] = -o
+        else:
+            offd[:, here] -= o
+        left = pair_cols(lambda c: af[p, :, c], t)
+        for n in range(4):
+            cols = slice(256 * n, 256 * n + 256)
+            u = three(nn, left, rs[p, hi_rows, cols], rs[p, lo_rows, cols])
+            if t == 0:
+                vt[p, :, cols] = u
+            else:
+                vt[p, :, cols] += u
+
+    def carry(p):
+        for n in range(4):
+            cols = slice(256 * n, 256 * n + 256)
+            qhi[p, :, cols], qlo[p, :, cols] = split(
+                three(nn, nthl[p], fhi[p, :, cols], flo[p, :, cols])
+            )
+
+    def late(t, p):
         w = weight[p]
-        size = 128 * len(blocks(t))
+        size, hi_rows, lo_rows, all_rows = span(t)
         here = slice(FIRST[t], FIRST[t] + size)
-        top, all_rows = slice(0, size), slice(0, 2 * size)
-        for k, b in enumerate(blocks(t)):
-            hi, lo = split(rg[p, b])
-            rhl[128 * k:128 * k + 128] = hi
-            rhl[size + 128 * k:size + 128 * k + 128] = lo
-        for n in range(2):
-            rows = slice(256 * n, 256 * n + 256)
-            g = three(nt, rhl[all_rows], whi[p, rows], wlo[p, rows])
-            ghl[top, rows], ghl[size:2 * size, rows] = split(g)
-        times = three(nt, rhl[all_rows], whi[p, WIDE:], wlo[p, WIDE:])
-        y = three(nn, ghl[all_rows], nhi[p], nlo[p])
-        up = y - times
-        o = three(nt, fohl[p], rhl[top], rhl[size:2 * size])
+        y = three(nt, rs[p, all_rows], qhi[p], qlo[p])
+        up = y - xs[p, here]
         if p == 0:
             ups[here] = w * up
-            offd[:, here] = -(w * o)
         else:
             ups[here] += w * up
-            offd[:, here] -= w * o
-        ath = pair_cols(lambda c: whi[p, WIDE:, c], t)
-        atl = pair_cols(lambda c: wlo[p, WIDE:, c], t)
-        at2 = jnp.concatenate([ath, atl], axis=0)
-        yth, ytl = split(jnp.transpose(y))
-        yt2 = jnp.concatenate([yth, ytl], axis=0)
-        fth = pair_cols(lambda c: whi[p, :WIDE, c], t)
-        ftl = pair_cols(lambda c: wlo[p, :WIDE, c], t)
-        m = three(nn, at2, ghl[top], ghl[size:2 * size]) - three(nt, yt2, fth, ftl)
+        for k, b in enumerate(blocks(t)):
+            vt[p, 0:256, lane(b)] -= jnp.transpose(y[128 * k:128 * k + 128])
+        at2 = jnp.concatenate(
+            [pair_cols(lambda c: af[p, 0:256, c], t), pair_cols(lambda c: af[p, 320:576, c], t)], axis=0
+        )
         uh, ul = split(up)
-        e = w * three(nn, at2, uh, ul)
-        fo2 = pair_cols(lambda c: fohl[p, :, c], t)
-        g2 = w * three(nn, fo2, ghl[top], ghl[size:2 * size])
-        if t == 0:
-            mt[p] = m
-        else:
-            mt[p] += m
-        low[...] -= e
-        diag[...] += g2
+        low[...] -= w * three(nn, at2, uh, ul)
+
+    def both(t, p):
+        early(t, p)
+        late(t, p)
 
     parts = {}
 
@@ -325,7 +342,7 @@
         else:
             add_part(name, n, lambda w: mids.at[n, w], lambda w, h: fins.at[n, w, h], src, out)
 
-    for t in range(3):
+    for t in (1, 2, 3):
         b1, b2 = blocks(t)
 
         def lr_out(q, h, b1=b1, b2=b2):
@@ -333,7 +350,7 @@
             return lr.at[m32((b1 + side * (b2 - b1)) * 128 + lax.rem(q, 2) * 64 + h * 32)]
 
         add_rows("lr%d" % t, t, lambda q, h, t=t: ups.at[m32(FIRST[t] + q * 64 + h * 32)], lr_out)
-    for t in (3, 4):
+    for t in (0, 4):
         b1 = blocks(t)[0]
         add_rows("lr%d" % t, t, lambda q, h, t=t: ups.at[m16(FIRST[t] + q * 32 + h * 16)],
                  lambda q, h, b1=b1: lr.at[m16(b1 * 128 + q * 32 + h * 16)], True)
@@ -343,7 +360,7 @@
                  lambda q, h, j=j: ln.at[m32(j * 256 + q * 64 + h * 32)])
     add_rows("ld", 7, lambda q, h: low.at[m32(q * 64 + h * 32)],
              lambda q, h: ld.at[m32(q * 64 + h * 32)])
-    for n, ts in ((8, slice(0, 768)), (9, slice(768, 1024))):
+    for n, ts in ((8, slice(0, 896)), (9, slice(896, 1024))):
         add_part("of%d" % n, n, lambda w, ts=ts: omid.at[w, :, ts],
                  lambda w, h, ts=ts: ofin.at[w, h, :, ts],
                  lambda q, h, ts=ts: offd.at[m8(q * 16 + h * 8), ts],
@@ -359,15 +376,20 @@
 
     def finish(p):
         w = weight[p]
-        mid = jnp.transpose(mt[p]) - dn[p]
-        if p == 0:
-            lnw[...] = w * mid
-        else:
-            lnw[...] += w * mid
-        ghl[:, 0:256], ghl[:, 256:512] = split(mid)
+        vhl[0:320], vhl[320:640] = split(vt[p])
+        for n in range(2):
+            rows = slice(256 * n, 256 * n + 256)
+            m = three(nt, vhl[...], fhi[p, rows], flo[p, rows])
+            diag[:, rows] += w * m[256:320]
+            mid = jnp.transpose(m[0:256]) - dn[p, rows]
+            if p == 0:
+                lnw[rows] = w * mid
+            else:
+                lnw[rows] += w * mid
+            mhl[p, rows, 0:256], mhl[p, rows, 256:512] = split(mid)
 
     def finish_low(p):
-        low[...] -= weight[p] * three(nn, nthl[p], ghl[:, 0:256], ghl[:, 256:512])
+        low[...] -= weight[p] * three(nn, nthl[p], mhl[p, :, 0:256], mhl[p, :, 256:512])
 
     def offdiag_out(ts):
         for t in ts:
@@ -391,93 +413,102 @@
     loads[0].wait()
     prep_a(0)
     event(1, 0)
+    prep_a(1)
     f_start(1)
-    prep_a(1)
-    event(1, 1)
-    f_relay(0)
     loads[1].wait()
     prep_n(0)
+    prep_n(1)
+    event(1, 1)
+    mate_wait(0)
+    early(0, 0)
     stage1("rb")
     event(1, 2)
-    prep_n(1)
+    f_relay(0)
+    early(0, 1)
+    event(1, 3)
     loads[2].wait()
     prep_d(0)
-    event(1, 3)
     stage2("rb")
-    f_last(0)
     prep_d(1)
+    event(2, 0)
     loads[3].wait()
     low[...] = weight[0] * lbuf[0] + weight[1] * lbuf[1]
     own_rows = pl.ds(pl.multiple_of(col * 64, 64), 64)
     diag[...] = weight[0] * dbuf[0, own_rows] + weight[1] * dbuf[1, own_rows]
-    event(2, 0)
+    mate_wait(1)
+    mate_wait(2)
+    early(1, 0)
+    event(2, 1)
+    f_last(0)
+    early(1, 1)
     f_relay(1)
+    event(2, 2)
     f_use(0)
-    mate_wait(0)
-    mate_wait(1)
-    piece(0, 0)
+    carry(0)
+    event(2, 3)
+    late(0, 0)
+    late(1, 0)
     stage3("rb")
-    event(2, 1)
+    event(3, 0)
     f_last(1)
-    event(2, 2)
+    mate_wait(3)
+    mate_wait(4)
+    early(2, 0)
+    event(3, 1)
     f_use(1)
-    event(2, 3)
-    piece(0, 1)
+    carry(1)
+    late(0, 1)
     stage0("lr0")
-    event(3, 0)
-    event(3, 1)
-    mate_wait(2)
-    mate_wait(3)
-    piece(1, 0)
-    stage1("lr0")
     event(4, 0)
     event(4, 1)
+    late(1, 1)
+    stage0("lr1")
+    early(2, 1)
+    stage1("lr0")
     cross(5)
     cross(6)
-    piece(1, 1)
-    stage0("lr1")
+    late(2, 0)
+    stage1("lr1")
     stage2("lr0")
     cross(7)
-    mate_wait(4)
+    late(2, 1)
+    stage0("lr2")
+    stage2("lr1")
+    stage3("lr0")
     mate_wait(5)
-    piece(2, 0)
-    stage1("lr1")
-    stage3("lr0")
-    piece(2, 1)
-    all_of(stage0, "lr2", "of8")
-    stage2("lr1")
     mate_wait(6)
-    piece(3, 0)
-    all_of(stage1, "lr2", "of8")
-    piece(3, 1)
-    stage0("lr3")
+    both(3, 0)
+    stage1("lr2")
     stage3("lr1")
+    both(3, 1)
+    all_of(stage0, "lr3", "of8")
+    stage2("lr2")
     mate_wait(7)
-    piece(4, 0)
-    all_of(stage2, "lr2", "of8")
-    stage1("lr3")
-    piece(4, 1)
-    all_of(stage0, "lr4", "nd", "of9")
+    both(4, 0)
+    all_of(stage1, "lr3", "of8")
+    stage3("lr2")
+    both(4, 1)
+    all_of(stage0, "lr4", "of9")
     finish(0)
-    stage2("lr3")
+    all_of(stage2, "lr3", "of8")
+    finish(1)
+    all_of(stage0, "ln0", "ln1", "nd")
     finish_low(0)
-    finish(1)
-    all_of(stage0, "ln0", "ln1")
-    all_of(stage3, "lr2", "of8")
-    all_of(stage1, "lr4", "nd", "of9")
     finish_low(1)
     stage0("ld")
-    stage3("lr3")
-    all_of(stage1, "ln0")
-    all_of(stage2, "lr4", "nd", "of9")
-    all_of(stage1, "ln1", "ld")
-    all_of(stage3, "lr4", "nd", "of9")
-    all_of(stage2, "ln0", "ln1", "ld")
+    all_of(stage1, "lr4", "of9")
+    all_of(stage3, "lr3", "of8")
+    all_of(stage1, "ln0", "ln1", "nd")
+    all_of(stage2, "lr4", "of9")
+    stage1("ld")
+    all_of(stage2, "ln0", "ln1")
+    all_of(stage3, "lr4", "of9")
+    all_of(stage2, "nd", "ld")
     stage4("of8")
-    offdiag_out(range(3))
-    all_of(stage3, "ln0", "ln1", "ld")
+    offdiag_out(range(4))
+    all_of(stage3, "ln0", "ln1", "nd", "ld")
     stage4("of9")
-    offdiag_out(range(3, 5))
+    offdiag_out(range(4, 5))
     all_of(stage4, "rb", "lr0", "lr1", "lr2", "lr3", "lr4", "nd", "ln0", "ln1", "ld")
     for copy in sent:
         copy.wait_send()
@@ -501,10 +532,12 @@
         out_specs=[pl.BlockSpec(memory_space=pltpu.VMEM)] * 6,
         scratch_shapes=[
             f32(2, WIDE, WIDE), f32(2, ROWS, LEAF), f32(2, WIDE, LEAF), f32(2, LEAF, LEAF),
-            f32(2, Z, 128, ROWS), f32(2, WIDE, ROWS), bf16(2, 128, ROWS),
-            bf16(2, WIDE + LEAF, ROWS), bf16(2, WIDE + LEAF, ROWS),
+            f32(2, Z, 128, ROWS), f32(2, WIDE, ROWS),
+            bf16(2, WIDE, ROWS), bf16(2, WIDE, ROWS), bf16(2, 640, ROWS),
+            bf16(2, LEAF, ROWS), bf16(2, LEAF, ROWS),
             bf16(2, WIDE, LEAF), bf16(2, WIDE, LEAF), bf16(2, 2 * LEAF, WIDE),
-            f32(2, WIDE, LEAF), f32(2, LEAF, WIDE), bf16(512, ROWS), bf16(512, WIDE),
+            f32(2, WIDE, LEAF), bf16(2, 2 * ROWS, ROWS), f32(2, ROWS, LEAF), f32(2, 320, ROWS),
+            bf16(640, ROWS), bf16(2, WIDE, 512),
             f32(ROWS, LEAF), f32(64, ROWS), f32(64, ROWS), f32(64, WIDE), f32(16, ROWS),
             f32(WIDE, LEAF), f32(LEAF, LEAF),
             f32(8, 2, 32, LEAF), f32(8, 2, 2, 32, LEAF), f32(2, 8, ROWS), f32(2, 2, 8, ROWS),
@@ -522,11 +555,15 @@
 
 
 def settle_kernel(*refs):
-    ins, outs, sems = refs[:6], refs[6:12], refs[12]
-    copies = [pltpu.make_async_copy(a, b, sems.at[k]) for k, (a, b) in enumerate(zip(ins, outs))]
-    for copy in copies:
+    ins, outs, bufs, sems = refs[:6], refs[6:12], refs[12:18], refs[18]
+    down = [pltpu.make_async_copy(a, b, sems.at[0, k]) for k, (a, b) in enumerate(zip(ins, bufs))]
+    up = [pltpu.make_async_copy(a, b, sems.at[1, k]) for k, (a, b) in enumerate(zip(bufs, outs))]
+    for copy in down:
         copy.start()
-    for copy in copies:
+    for first, second in zip(down, up):
+        first.wait()
+        second.start()
+    for copy in up:
         copy.wait()
 
 
@@ -536,7 +573,7 @@
         out_shape=tuple(jax.ShapeDtypeStruct(shape, F32) for shape in SHAPES),
         in_specs=[pl.BlockSpec(memory_space=pl.ANY)] * 6,
         out_specs=[pl.BlockSpec(memory_space=pl.ANY)] * 6,
-        scratch_shapes=[pltpu.SemaphoreType.DMA((6,))],
+        scratch_shapes=[pltpu.VMEM(shape, F32) for shape in SHAPES] + [pltpu.SemaphoreType.DMA((2, 6))],
     )(*arrays)
 
 

time: 175 us -> 105 us (0.60)
  Pallas kernels: 173 us -> 104 us
    pallas_call x1, Pallas kernels: 70.6 us -> 2.73 us  [settle(): pl.pallas_call(settle_kernel, out_shape=tuple((jax.ShapeDtypeStruct(shape...]
    pallas_call x1, Pallas kernels: 103 us -> 101 us  [sweep(): pl.pallas_call(kernel, out_shape=tuple((jax.ShapeDtypeStruct(shape, F32)...]
where the time goes in v4:
time: 105 us; the launch traced here: 104 us
  Pallas kernels  104 us (99%)
    pallas_call x1, Pallas kernels, sweep(): pl.pallas_call(kernel, out_shape=tuple((jax.ShapeDtypeStruct(shape, F32)...  101 us
    pallas_call x1, Pallas kernels, settle(): pl.pallas_call(settle_kernel, out_shape=tuple((jax.ShapeDtypeStruct(shape...  2.73 us

profile of v4, /device:TPU:6, one launch (start us, length us, event | category | flops | bytes accessed | tf_op | source)
XLA Modules:
  0.0 104.4 jit_solution(12558464624184607705)
XLA Ops:
  0.6 100.8 %shard_map.127 = (f32[16,1024]{1,0:T(8,128)}, f32[64,1024]{1,0:T(8,128)}, f32[64,512]{1,0:T(8,128)}, f32[1024,256]{1,0:T(8,128)}, f32[512,256]{1,0:T(8,128)}, /*index=5*/f32[256,256]{1,0:T(8,128)}) custom-call(s32[1,8]{1,0:T(1,128)} %pat.1, f32[2]{0:T(128)} %weight.1, f32[2,16,1024]{2,1,0:T(8,128)} %r_ref.1, f32[2,64,1024]{2,1,0:T(8,128)} %bitcast.17, ...), custom_call_target="tpu_custom_call" | custom-call | tf_op jit(solution)/shard_map/pallas_call | solution.py:526
  101.4 2.7 %shard_map.128 = (f32[16,1024]{1,0:T(8,128)}, f32[64,1024]{1,0:T(8,128)}, f32[64,512]{1,0:T(8,128)}, f32[1024,256]{1,0:T(8,128)}, f32[512,256]{1,0:T(8,128)}, /*index=5*/f32[256,256]{1,0:T(8,128)}) custom-call(f32[16,1024]{1,0:T(8,128)} %get-tuple-element.18.refs_0_, f32[64,1024]{1,0:T(8,128)} %get-tuple-element.19.refs_1_, ...), custom_call_target="tpu_custom_call" | custom-call | tf_op jit(solution)/shard_map/pallas_call | solution.py:571

commit v5 on v4

--- a/solution.py
+++ b/solution.py
@@ -223,7 +223,7 @@
         cols = [get(lane(b)) for b in blocks(t)]
         return cols[0] if len(cols) == 1 else jnp.concatenate(cols, axis=1)
 
-    def early(t, p):
+    def early(t, p, first):
         size, hi_rows, lo_rows, all_rows = span(t)
         here = slice(FIRST[t], FIRST[t] + size)
         for k, b in enumerate(blocks(t)):
@@ -232,7 +232,7 @@
         xs[p, here] = three(nt, rs[p, all_rows], af[p, 0:256], af[p, 320:576])
         fo = jnp.concatenate([af[p, 256:320], af[p, 576:640]], axis=0)
         o = weight[p] * three(nt, fo, rs[p, hi_rows], rs[p, lo_rows])
-        if p == 0:
+        if first:
             offd[:, here] = -o
         else:
             offd[:, here] -= o
@@ -252,13 +252,13 @@
                 three(nn, nthl[p], fhi[p, :, cols], flo[p, :, cols])
             )
 
-    def late(t, p):
+    def late(t, p, first):
         w = weight[p]
         size, hi_rows, lo_rows, all_rows = span(t)
         here = slice(FIRST[t], FIRST[t] + size)
         y = three(nt, rs[p, all_rows], qhi[p], qlo[p])
         up = y - xs[p, here]
-        if p == 0:
+        if first:
             ups[here] = w * up
         else:
             ups[here] += w * up
@@ -270,9 +270,9 @@
         uh, ul = split(up)
         low[...] -= w * three(nn, at2, uh, ul)
 
-    def both(t, p):
-        early(t, p)
-        late(t, p)
+    def both(t, p, first):
+        early(t, p, first)
+        late(t, p, first)
 
     parts = {}
 
@@ -374,12 +374,14 @@
     add_part("rb", 11, lambda w: rmid.at[w], lambda w, h: rfin.at[w, h],
              lambda q, h: rootw.at[:, lanes(q, h)], lambda q, h: rb.at[:, lanes(q, h)])
 
-    def finish(p):
-        w = weight[p]
-        vhl[0:320], vhl[320:640] = split(vt[p])
-        for n in range(2):
-            rows = slice(256 * n, 256 * n + 256)
-            m = three(nt, vhl[...], fhi[p, rows], flo[p, rows])
+    def close(p):
+        vhl[p, 0:320], vhl[p, 320:640] = split(vt[p])
+
+    def finish(n):
+        rows = slice(256 * n, 256 * n + 256)
+        for p in range(2):
+            w = weight[p]
+            m = three(nt, vhl[p], fhi[p, rows], flo[p, rows])
             diag[:, rows] += w * m[256:320]
             mid = jnp.transpose(m[0:256]) - dn[p, rows]
             if p == 0:
@@ -420,11 +422,11 @@
     prep_n(1)
     event(1, 1)
     mate_wait(0)
-    early(0, 0)
+    early(0, 0, True)
     stage1("rb")
     event(1, 2)
     f_relay(0)
-    early(0, 1)
+    early(0, 1, False)
     event(1, 3)
     loads[2].wait()
     prep_d(0)
@@ -437,62 +439,65 @@
     diag[...] = weight[0] * dbuf[0, own_rows] + weight[1] * dbuf[1, own_rows]
     mate_wait(1)
     mate_wait(2)
-    early(1, 0)
+    early(1, 0, True)
     event(2, 1)
     f_last(0)
-    early(1, 1)
+    early(1, 1, False)
     f_relay(1)
     event(2, 2)
     f_use(0)
     carry(0)
     event(2, 3)
-    late(0, 0)
-    late(1, 0)
+    late(0, 0, True)
+    late(1, 0, True)
     stage3("rb")
     event(3, 0)
     f_last(1)
     mate_wait(3)
     mate_wait(4)
-    early(2, 0)
+    early(2, 0, True)
     event(3, 1)
     f_use(1)
     carry(1)
-    late(0, 1)
+    late(0, 1, False)
     stage0("lr0")
     event(4, 0)
     event(4, 1)
-    late(1, 1)
+    early(2, 1, False)
+    late(1, 1, False)
     stage0("lr1")
-    early(2, 1)
     stage1("lr0")
     cross(5)
     cross(6)
-    late(2, 0)
+    late(2, 0, True)
     stage1("lr1")
     stage2("lr0")
     cross(7)
-    late(2, 1)
+    late(2, 1, False)
     stage0("lr2")
     stage2("lr1")
     stage3("lr0")
+    both(3, core, True)
+    stage1("lr2")
+    stage3("lr1")
     mate_wait(5)
     mate_wait(6)
-    both(3, 0)
-    stage1("lr2")
-    stage3("lr1")
-    both(3, 1)
+    both(3, other, False)
     all_of(stage0, "lr3", "of8")
     stage2("lr2")
-    mate_wait(7)
-    both(4, 0)
+    both(4, core, True)
     all_of(stage1, "lr3", "of8")
     stage3("lr2")
-    both(4, 1)
+    mate_wait(7)
+    both(4, other, False)
     all_of(stage0, "lr4", "of9")
+    close(0)
+    close(1)
+    all_of(stage2, "lr3", "of8")
     finish(0)
-    all_of(stage2, "lr3", "of8")
+    stage0("ln0")
     finish(1)
-    all_of(stage0, "ln0", "ln1", "nd")
+    all_of(stage0, "ln1", "nd")
     finish_low(0)
     finish_low(1)
     stage0("ld")
@@ -525,7 +530,7 @@
     n = 12
     return pl.pallas_call(
         kernel,
-        out_shape=tuple(jax.ShapeDtypeStruct(shape, F32) for shape in SHAPES),
+        out_shape=tuple(pltpu.VMEM(shape, F32) for shape in SHAPES),
         in_specs=[pl.BlockSpec(memory_space=pltpu.SMEM)] * 2
         + [pl.BlockSpec(memory_space=pltpu.VMEM)] * 2
         + [pl.BlockSpec(memory_space=pl.ANY)] * 4,
@@ -537,7 +542,7 @@
             bf16(2, LEAF, ROWS), bf16(2, LEAF, ROWS),
             bf16(2, WIDE, LEAF), bf16(2, WIDE, LEAF), bf16(2, 2 * LEAF, WIDE),
             f32(2, WIDE, LEAF), bf16(2, 2 * ROWS, ROWS), f32(2, ROWS, LEAF), f32(2, 320, ROWS),
-            bf16(640, ROWS), bf16(2, WIDE, 512),
+            bf16(2, 640, ROWS), bf16(2, WIDE, 512),
             f32(ROWS, LEAF), f32(64, ROWS), f32(64, ROWS), f32(64, WIDE), f32(16, ROWS),
             f32(WIDE, LEAF), f32(LEAF, LEAF),
             f32(8, 2, 32, LEAF), f32(8, 2, 2, 32, LEAF), f32(2, 8, ROWS), f32(2, 2, 8, ROWS),
@@ -555,15 +560,11 @@
 
 
 def settle_kernel(*refs):
-    ins, outs, bufs, sems = refs[:6], refs[6:12], refs[12:18], refs[18]
-    down = [pltpu.make_async_copy(a, b, sems.at[0, k]) for k, (a, b) in enumerate(zip(ins, bufs))]
-    up = [pltpu.make_async_copy(a, b, sems.at[1, k]) for k, (a, b) in enumerate(zip(bufs, outs))]
-    for copy in down:
+    ins, outs, sems = refs[:6], refs[6:12], refs[12]
+    copies = [pltpu.make_async_copy(a, b, sems.at[k]) for k, (a, b) in enumerate(zip(ins, outs))]
+    for copy in copies:
         copy.start()
-    for first, second in zip(down, up):
-        first.wait()
-        second.start()
-    for copy in up:
+    for copy in copies:
         copy.wait()
 
 
@@ -571,10 +572,10 @@
     return pl.pallas_call(
         settle_kernel,
         out_shape=tuple(jax.ShapeDtypeStruct(shape, F32) for shape in SHAPES),
-        in_specs=[pl.BlockSpec(memory_space=pl.ANY)] * 6,
+        in_specs=[pl.BlockSpec(memory_space=pltpu.VMEM)] * 6,
         out_specs=[pl.BlockSpec(memory_space=pl.ANY)] * 6,
-        scratch_shapes=[pltpu.VMEM(shape, F32) for shape in SHAPES] + [pltpu.SemaphoreType.DMA((2, 6))],
-    )(*arrays)
+        scratch_shapes=[pltpu.SemaphoreType.DMA((6,))],
+    )(*(pltpu.with_memory_space_constraint(array, pltpu.VMEM) for array in arrays))
 
 
 def shards(

time: 105 us -> 101 us (0.962)
  Pallas kernels: 104 us -> 100 us
    pallas_call x1, Pallas kernels: 101 us -> 98.6 us  [sweep(): pl.pallas_call(kernel, out_shape=tuple((pltpu.VMEM(shape, F32) for shape...]
    pallas_call x1, Pallas kernels: 2.73 us -> 1.43 us  [settle(): pl.pallas_call(settle_kernel, out_shape=tuple((jax.ShapeDtypeStruct(shape...]
where the time goes in v5:
time: 101 us
  Pallas kernels  100 us (99%)
    pallas_call x1, Pallas kernels, sweep(): pl.pallas_call(kernel, out_shape=tuple((pltpu.VMEM(shape, F32) for shape...  98.6 us

profile of v5, /device:TPU:6, one launch (start us, length us, event | category | flops | bytes accessed | tf_op | source)
XLA Modules:
  0.0 100.9 jit_solution(6334445149137746359)
XLA Ops:
  0.6 98.6 %shard_map.127 = (f32[16,1024]{1,0:T(8,128)S(1)}, f32[64,1024]{1,0:T(8,128)S(1)}, f32[64,512]{1,0:T(8,128)S(1)}, f32[1024,256]{1,0:T(8,128)S(1)}, f32[512,256]{1,0:T(8,128)S(1)}, /*index=5*/f32[256,256]{1,0:T(8,128)S(1)}) custom-call(s32[1,8]{1,0:T(1,128)} %pat.1, f32[2]{0:T(128)} %weight.1, f32[2,16,1024]{2,1,0:T(8,128)} %r_ref.1, f32[2,64,1024]{2,1,0:T(8,128)} %bitcast.17, ...), custom_call_target="tpu_custom_call" | custom-call | tf_op jit(solution)/shard_map/pallas_call | solution.py:531
  99.3 1.4 %shard_map.128 = (f32[16,1024]{1,0:T(8,128)}, f32[64,1024]{1,0:T(8,128)}, f32[64,512]{1,0:T(8,128)}, f32[1024,256]{1,0:T(8,128)}, f32[512,256]{1,0:T(8,128)}, /*index=5*/f32[256,256]{1,0:T(8,128)}) custom-call(f32[16,1024]{1,0:T(8,128)S(1)} %get-tuple-element.18.refs_0_, f32[64,1024]{1,0:T(8,128)S(1)} %get-tuple-element.19.refs_1_, ...), custom_call_target="tpu_custom_call" | custom-call | tf_op jit(solution)/shard_map/pallas_call | solution.py:572

commit v6 on v5

--- a/solution.py
+++ b/solution.py
@@ -496,13 +496,13 @@
     all_of(stage2, "lr3", "of8")
     finish(0)
     stage0("ln0")
+    all_of(stage1, "lr4", "of9")
     finish(1)
     all_of(stage0, "ln1", "nd")
+    all_of(stage3, "lr3", "of8")
     finish_low(0)
     finish_low(1)
     stage0("ld")
-    all_of(stage1, "lr4", "of9")
-    all_of(stage3, "lr3", "of8")
     all_of(stage1, "ln0", "ln1", "nd")
     all_of(stage2, "lr4", "of9")
     stage1("ld")

time: 101 us -> 102 us (level)
  no operation moved by 1% of the time
where the time goes in v6:
time: 102 us
  Pallas kernels  101 us (99%)
    pallas_call x1, Pallas kernels, sweep(): pl.pallas_call(kernel, out_shape=tuple((pltpu.VMEM(shape, F32) for shape...  99.3 us

profile of v6, /device:TPU:6, one launch (start us, length us, event | category | flops | bytes accessed | tf_op | source)
XLA Modules:
  0.0 101.5 jit_solution(3485937265170274902)
XLA Ops:
  0.6 99.3 %shard_map.127 = (f32[16,1024]{1,0:T(8,128)S(1)}, f32[64,1024]{1,0:T(8,128)S(1)}, f32[64,512]{1,0:T(8,128)S(1)}, f32[1024,256]{1,0:T(8,128)S(1)}, f32[512,256]{1,0:T(8,128)S(1)}, /*index=5*/f32[256,256]{1,0:T(8,128)S(1)}) custom-call(s32[1,8]{1,0:T(1,128)} %pat.1, f32[2]{0:T(128)} %weight.1, f32[2,16,1024]{2,1,0:T(8,128)} %r_ref.1, f32[2,64,1024]{2,1,0:T(8,128)} %bitcast.17, ...), custom_call_target="tpu_custom_call" | custom-call | tf_op jit(solution)/shard_map/pallas_call | solution.py:531
  99.9 1.4 %shard_map.128 = (f32[16,1024]{1,0:T(8,128)}, f32[64,1024]{1,0:T(8,128)}, f32[64,512]{1,0:T(8,128)}, f32[1024,256]{1,0:T(8,128)}, f32[512,256]{1,0:T(8,128)}, /*index=5*/f32[256,256]{1,0:T(8,128)}) custom-call(f32[16,1024]{1,0:T(8,128)S(1)} %get-tuple-element.18.refs_0_, f32[64,1024]{1,0:T(8,128)S(1)} %get-tuple-element.19.refs_1_, ...), custom_call_target="tpu_custom_call" | custom-call | tf_op jit(solution)/shard_map/pallas_call | solution.py:572
